TPU v7x, 128 devices: a whole 4x4x4 slice. The times are simulated.
128 devices in a mesh: row: 8 (over y, z_lo), col: 16 (over z_hi, x, core).
Axes of the slice: x: 4, y: 4, z: 4 (z_hi: 2, z_lo: 2; z = z_hi * 2 + z_lo), core: 2. Of those that a mesh axis runs over, the one named last changes fastest.
Arguments:
- kernel: bfloat16 [20480, 20480], P('row', 'col'), may hold values from -2.861023e-06 to 2.861023e-06
- occ: bfloat16 [20480, 128], P(('row', 'col')), may hold values from -6 to 6
- virt: bfloat16 [20480, 512], P(('col', 'row')), may hold values from -6 to 6
- rhs: float32 [128, 512], replicated, may hold values from -6 to 6
- e_occ: float32 [128], replicated, may hold values from -2 to -0.5
- e_virt: float32 [512], replicated, may hold values from 0.2 to 3
Outputs:
- amplitudes: float32 [128, 512], replicated
All inputs are finite; a program needn't handle non-finite values.
Results may differ from a plain program's by a relative error of at most 0.0045.
Values may be sent and summed in bfloat16 or wider, within the bound.
No kernel may reach another device: no remote copies, remote signals or barrier semaphores. Data moves between devices by JAX's collectives and lax.ppermute only.
A program may use at most 64 MiB of HBM per device.

v0:
```python
import math

import jax
import jax.numpy as jnp
from jax import lax
from jax.sharding import PartitionSpec as P

ITERS = 2


def in_order(pieces, dim):
    pieces = jnp.moveaxis(pieces, 0, dim)
    dims = pieces.shape
    return pieces.reshape(*dims[:dim], dims[dim] * dims[dim + 1], *dims[dim + 2 :])


def sent_to_all(shard, axis):
    peers = lax.axis_size(axis)
    return lax.all_to_all(
        jnp.broadcast_to(shard[None], (peers, *shard.shape)), axis, 0, 0, tiled=True
    )


def gather_directly(shard, axis, dim):
    return in_order(sent_to_all(shard, axis), dim)


def body(kernel, occ, virt, rhs, e_occ, e_virt):
    denom = e_virt[None, :] - e_occ[:, None]
    amplitudes = rhs / denom
    virt_cols = gather_directly(virt, "row", 0)
    occ_full = lax.all_gather(occ, "col", axis=0, tiled=True)

    def fold(total, pieces, start):
        resp_rows, occ_piece = pieces
        kern_rows = lax.dynamic_slice_in_dim(kernel, start, resp_rows.shape[0], 0)
        outer = lax.dot_general(
            resp_rows, virt_cols, (((1,), (1,)), ((), ())), preferred_element_type=jnp.float32
        )
        weighted = (kern_rows.astype(jnp.float32) * outer).astype(jnp.bfloat16)
        return total + lax.dot_general(
            occ_piece, weighted, (((0,), (0,)), ((), ())), preferred_element_type=jnp.float32
        )

    for step in range(ITERS):
        amp_b = amplitudes.astype(jnp.bfloat16)
        empty = jnp.zeros((occ.shape[1], virt_cols.shape[0]), jnp.float32)
        resp_full = jnp.dot(occ_full, amp_b, preferred_element_type=jnp.float32).astype(
            jnp.bfloat16
        )
        height = occ_full.shape[0]
        block = math.gcd(height, 512)

        def add_block(index, total):
            start = (index * block).astype(jnp.int32)
            pieces = (
                lax.dynamic_slice_in_dim(resp_full, start, block, 0),
                lax.dynamic_slice_in_dim(occ_full, start, block, 0),
            )
            return fold(total, pieces, start)

        partial_sum = lax.fori_loop(0, height // block, add_block, empty)
        projection = jnp.dot(
            partial_sum, virt_cols.astype(jnp.float32), precision=lax.Precision.HIGHEST
        )
        exchange = lax.psum(projection, ("row", "col"))
        amplitudes = (rhs - exchange) / denom
    return amplitudes


def solution(mesh):
    in_specs = (P("row", "col"), P(("row", "col"), None), P(("col", "row"), None), P(), P(), P())
    out_specs = P()
    return jax.shard_map(body, mesh=mesh, in_specs=in_specs, out_specs=out_specs, check_vma=False)
```

profile of v0, /device:TPU:1, one launch (start us, length us, event | category | flops | bytes accessed | tf_op | source)
XLA Modules:
  0.0 371.0 jit_solution(7374602793152194372)
XLA Ops:
  6.5 0.0 copy-start.1
  6.5 0.0 copy-start
  6.5 0.0 copy-start.3
  6.5 0.0 copy-start.2
  6.5 2.1 broadcast_in_dim.2
  8.7 6.4 %all-to-all-start = ((bf16[8,160,512]{2,1,0:T(8,128)(2,1)}), bf16[8,160,512]{2,1,0:T(8,128)(2,1)S(1)}, u32[]{:S(2)}, u32[]{:S(2)}) async-start(bf16[8,160,512]{2,1,0:T(8,128)(2,1)} %broadcast_in_dim.2), calls=%async_computation | async-start | bytes 2621440 | tf_op jit(solution)/shard_map/all_to_all | solution.py:19
  15.0 0.0 all-reduce.3.cloned.1.call-start
  15.1 0.0 copy-done.1
  15.1 28.9 %all_gather.3 = bf16[2560,128]{1,0:T(8,128)(2,1)S(1)} all-gather(bf16[160,128]{1,0:T(8,128)(2,1)S(1)} %copy-done.1), channel_id=1, replica_groups=mesh['row'=8,'col'=16] {'col'}, dimensions={0}, use_global_device_ids=true | all-gather | bytes 696320 | tf_op jit(solution)/shard_map/all_gather | solution.py:32
  44.0 0.0 copy-done
  44.0 0.0 copy-done.3
  44.0 0.0 copy-done.2
  44.0 2.4 fusion.14
  46.5 0.0 all-to-all-done
  46.5 14.5 %while.28 = (s32[]{:T(128)}, f32[128,1280]{1,0:T(8,128)S(1)}, bf16[2560,128]{1,0:T(8,128)(2,1)S(1)}, bf16[2560,1280]{1,0:T(8,128)(2,1)}, bf16[2560,512]{1,0:T(8,...) while((s32[]{:T(128)}, f32[128,1280]{1,0:T(8,128)S(1)}, ...), condition=%wide.region_1.0_spmd.clone, body=%wide.region_0.0_spmd.clone.sunk | while | flops 841154560 | bytes 4589724 | solution.py:62
  46.5 2.9 convolution_add_fusion.4
  49.4 2.9 convolution_add_fusion.4
  52.3 2.9 convolution_add_fusion.4
  55.2 2.9 convolution_add_fusion.4
  58.1 2.9 convolution_add_fusion.4
  61.0 1.4 fusion.24
  62.4 0.0 all-reduce.3.cloned.1.call-update
  62.4 0.0 all-reduce.5.cloned.1.call-start
  62.5 139.9 %all-reduce.3.cloned.1.call-done = f32[128,512]{1,0:T(8,128)} async-done(((f32[128,512]{1,0:T(8,128)}), f32[128,512]{1,0:T(8,128)}) %all-reduce.3.cloned.1.call-update) | async-done | bytes 262160 | tf_op jit(solution)/shard_map/psum | solution.py:66
  202.4 3.4 fusion.15
  205.8 14.5 %while.29 = (s32[]{:T(128)}, f32[128,1280]{1,0:T(8,128)S(1)}, bf16[2560,128]{1,0:T(8,128)(2,1)S(1)}, bf16[2560,1280]{1,0:T(8,128)(2,1)}, bf16[2560,512]{1,0:T(8,...) while((s32[]{:T(128)}, f32[128,1280]{1,0:T(8,128)S(1)}, ...), condition=%wide.region_4.0_spmd.clone, body=%wide.region_3.0_spmd.clone.sunk | while | flops 841154560 | bytes 4589724 | solution.py:62
  205.8 2.9 convolution_add_fusion.5
  208.7 2.9 convolution_add_fusion.5
  211.6 2.9 convolution_add_fusion.5
  214.5 2.9 convolution_add_fusion.5
  217.4 2.9 convolution_add_fusion.5
  220.3 1.4 fusion.25
  221.7 0.0 all-reduce.5.cloned.1.call-update
  221.7 140.7 %all-reduce.5.cloned.1.call-done = f32[128,512]{1,0:T(8,128)} async-done(((f32[128,512]{1,0:T(8,128)}), f32[128,512]{1,0:T(8,128)}) %all-reduce.5.cloned.1.call-update) | async-done | bytes 262160 | tf_op jit(solution)/shard_map/psum | solution.py:66
  362.4 1.8 subtract_divide_fusion
  (2 shorter events, 0.0 us)
Async XLA Ops:
  6.5 8.6 %copy-start.1 = (bf16[160,128]{1,0:T(8,128)(2,1)S(1)}, bf16[160,128]{1,0:T(8,128)(2,1)}, u32[]{:S(2)}) copy-start(bf16[160,128]{1,0:T(8,128)(2,1)} %param.11) | copy-start | bytes 122884
  6.5 37.5 %copy-start = (f32[128,512]{1,0:T(8,128)S(1)}, f32[128,512]{1,0:T(8,128)}, u32[]{:S(2)}) copy-start(f32[128,512]{1,0:T(8,128)} %param.13) | copy-start | bytes 786436
  6.5 37.5 %copy-start.3 = (f32[128]{0:T(128)S(1)}, f32[128]{0:T(128)}, u32[]{:S(2)}) copy-start(f32[128]{0:T(128)} %param.14) | copy-start | bytes 1540
  6.5 37.5 %copy-start.2 = (f32[512]{0:T(512)S(1)}, f32[512]{0:T(512)}, u32[]{:S(2)}) copy-start(f32[512]{0:T(512)} %param.15) | copy-start | bytes 6148
  8.7 37.8 %all-to-all-start = ((bf16[8,160,512]{2,1,0:T(8,128)(2,1)}), bf16[8,160,512]{2,1,0:T(8,128)(2,1)S(1)}, u32[]{:S(2)}, u32[]{:S(2)}) async-start(bf16[8,160,512]{2,1,0:T(8,128)(2,1)} %broadcast_in_dim.2), calls=%async_computation | async-start | bytes 2621440 | tf_op jit(solution)/shard_map/all_to_all | solution.py:19
  15.0 187.4 %all-reduce.3.cloned.1.call-start = ((), (), s32[]{:S(2)}) async-start(), calls=%async_computation.1 | async-start | bytes 524288 | tf_op jit(solution)/shard_map/psum | solution.py:66
  62.4 300.0 %all-reduce.5.cloned.1.call-start = ((), (), s32[]{:S(2)}) async-start(), calls=%async_computation.2 | async-start | bytes 524288 | tf_op jit(solution)/shard_map/psum | solution.py:66
Sparse Core Ops, SparseCore 0:
  62.5 139.8 all-reduce.2
  221.9 140.5 all-reduce.4
where the time goes:
time: 372 us; the launch traced here: 371 us
  waiting for transfers between devices  281 us (76%)
  matrix products  37.4 us (10%)
  blocking collectives  28.9 us (8%)
  between operations  13.5 us (4%)
  starting transfers between devices  6.44 us (2%)
    psum x2, waiting for transfers between devices, body(): exchange = lax.psum(projection, ('row', 'col'))  281 us
    all_gather x1, blocking collectives, body(): occ_full = lax.all_gather(occ, 'col', axis=0, tiled=True)  28.9 us
    dot_general x10, matrix products, fold(): lax.dot_general(occ_piece, weighted, (((0,), (0,)), ((), ())), preferred_...  28.8 us
  transfers between devices with their start and end apart: 3, of which 2 were waited for; matrix products, arithmetic and copies ran while one was open for 1% of the time, Pallas kernels for 0%

commit v1 on v0

v1 whole, which is shorter than its diff:
```python
import functools

import jax
import jax.numpy as jnp
from jax import lax
from jax.experimental import pallas as pl
from jax.experimental.pallas import tpu as pltpu
from jax.sharding import PartitionSpec as P

ITERS = 2
LANES = 128
BOTH = ("row", "col")


def sent_to_all(shard, axis):
    peers = lax.axis_size(axis)
    return lax.all_to_all(
        jnp.broadcast_to(shard[None], (peers, *shard.shape)), axis, 0, 0, tiled=True
    )


def gathered(shard, axis):
    pieces = sent_to_all(shard, axis)
    return pieces.reshape(pieces.shape[0] * pieces.shape[1], *pieces.shape[2:])


def response_kernel(wide, amp_ref, virt_ref, occ_ref, occ_t_ref, kern_ref, out_ref, w_ref, total_ref):
    step = pl.program_id(0)
    cols = virt_ref.shape[0]
    nt = (((1,), (1,)), ((), ()))
    f32, b16 = jnp.float32, jnp.bfloat16

    @pl.when(step == 0)
    def _():
        for start in range(0, cols, wide):
            here = pl.ds(start, wide)
            w_ref[:, here] = lax.dot_general(
                amp_ref[...], virt_ref[here, :], nt, preferred_element_type=f32
            ).astype(b16)
        total_ref[...] = jnp.zeros_like(total_ref)

    for start in range(0, cols, wide):
        here = pl.ds(start, wide)
        outer = jnp.dot(occ_ref[...], w_ref[:, here], preferred_element_type=f32)
        weighted = (kern_ref[:, here].astype(f32) * outer).astype(b16)
        total_ref[:, here] += jnp.dot(occ_t_ref[...], weighted, preferred_element_type=f32)

    @pl.when(step == pl.num_programs(0) - 1)
    def _():
        total = total_ref[...]
        high = total.astype(b16)
        low = (total - high.astype(f32)).astype(b16)
        exchange = jnp.dot(high, virt_ref[...], preferred_element_type=f32)
        exchange += jnp.dot(low, virt_ref[...], preferred_element_type=f32)
        out_ref[...] = exchange.astype(out_ref.dtype)


def partial_exchange(amp_b, virt_cols, occ_rows, occ_t, kernel):
    occupied, virtual = amp_b.shape
    rows, cols = kernel.shape
    height, wide = 512, 256
    whole = lambda *dims: pl.BlockSpec(dims, lambda s: (0, 0))
    return pl.pallas_call(
        functools.partial(response_kernel, wide),
        out_shape=jax.ShapeDtypeStruct((occupied, virtual), jnp.bfloat16),
        grid=(rows // height,),
        in_specs=[
            whole(occupied, virtual),
            whole(cols, virtual),
            pl.BlockSpec((height, occupied), lambda s: (s, 0)),
            pl.BlockSpec((occupied, height), lambda s: (0, s)),
            pl.BlockSpec((height, cols), lambda s: (s, 0)),
        ],
        out_specs=whole(occupied, virtual),
        scratch_shapes=[
            pltpu.VMEM((occupied, cols), jnp.bfloat16),
            pltpu.VMEM((occupied, cols), jnp.float32),
        ],
        compiler_params=pltpu.CompilerParams(
            dimension_semantics=("arbitrary",), vmem_limit_bytes=40 << 20
        ),
    )(amp_b, virt_cols, occ_rows, occ_t, kernel)


def body(kernel, occ, virt, rhs, e_occ, e_virt):
    occupied, virtual = rhs.shape
    split = (occupied, virtual // LANES, LANES)
    mine = lax.axis_index("row") * lax.axis_size("col") + lax.axis_index("col")
    virt_cols = gathered(virt, "row")
    occ_rows = gathered(occ, "col")
    occ_t = occ_rows.T
    rhs_mine = lax.dynamic_index_in_dim(rhs, mine, 0, False).reshape(split[1:])
    denom_mine = e_virt.reshape(split[1:]) - lax.dynamic_index_in_dim(e_occ, mine, 0, False)

    amp_b = (rhs / (e_virt[None, :] - e_occ[:, None])).astype(jnp.bfloat16)
    for step in range(ITERS):
        part = partial_exchange(amp_b, virt_cols, occ_rows, occ_t, kernel)
        parts = lax.all_to_all(part.reshape(split), BOTH, 0, 0, tiled=True)
        exchange = jnp.sum(parts.astype(jnp.float32), axis=0)
        amp_mine = (rhs_mine - exchange) / denom_mine
        if step < ITERS - 1:
            amp_b = sent_to_all(amp_mine.astype(jnp.bfloat16), BOTH).reshape(rhs.shape)
    return sent_to_all(amp_mine, BOTH).reshape(rhs.shape)


def solution(mesh):
    in_specs = (P("row", "col"), P(("row", "col"), None), P(("col", "row"), None), P(), P(), P())
    return jax.shard_map(body, mesh=mesh, in_specs=in_specs, out_specs=P(), check_vma=False)
```

time: 372 us -> 135 us (0.36)
  waiting for transfers between devices: 281 us -> 29 us
  matrix products: 37.4 us -> 0 us
  blocking collectives: 28.9 us -> 65.6 us
  Pallas kernels: 0 us -> 18.1 us
  between operations: 13.5 us -> 0.12 us
  local copies, waits for them, and re-layouts: 2.15 us -> 10.2 us
    psum x2 -> x0, waiting for transfers between devices: 281 us -> none  [body(): exchange = lax.psum(projection, ('row', 'col'))]
    all_to_all x0 -> x4, blocking collectives: none -> 65.6 us  [the longest x3 51.4 us: sent_to_all(): lax.all_to_all(jnp.broadcast_to(shard[None], (peers, *shard.shape)), axis...]
    dot_general x14 -> x0, matrix products: 37.4 us -> none  [the longest x10 28.8 us: fold(): lax.dot_general(occ_piece, weighted, (((0,), (0,)), ((), ())), preferred_...]
    all_gather x1 -> x0, blocking collectives: 28.9 us -> none  [body(): occ_full = lax.all_gather(occ, 'col', axis=0, tiled=True)]
    all_to_all x1, waiting for transfers between devices: 0.01 us -> 19.3 us  [sent_to_all(): lax.all_to_all(jnp.broadcast_to(shard[None], (peers, *shard.shape)), axis...]
    pallas_call x0 -> x2, Pallas kernels: none -> 18.1 us  [partial_exchange(): pl.pallas_call(functools.partial(response_kernel, wide), out_shape=jax.Sh...]
    all_to_all x0 -> x1, waiting for transfers between devices: none -> 9.68 us  [body(): parts = lax.all_to_all(part.reshape(split), BOTH, 0, 0, tiled=True)]
    unnamed x8 -> x14, local copies, waits for them, and re-layouts: 0.01 us -> 6.47 us
  transfers between devices with their start and end apart: 3 -> 2, of which waited for: 2 -> 2; matrix products, arithmetic and copies ran while one was open for 1% -> 1% of each run, Pallas kernels for 0% -> 0%
where the time goes in v1:
time: 135 us; the launch traced here: 134 us
  blocking collectives  65.6 us (49%)
  waiting for transfers between devices  29 us (21%)
  Pallas kernels  18.1 us (13%)
  local copies, waits for them, and re-layouts  10.2 us (8%)
  starting transfers between devices  9.62 us (7%)
  other arithmetic  1.64 us (1%)
    all_to_all x3, blocking collectives, sent_to_all(): lax.all_to_all(jnp.broadcast_to(shard[None], (peers, *shard.shape)), axis...  51.4 us
    all_to_all x1, waiting for transfers between devices, sent_to_all(): lax.all_to_all(jnp.broadcast_to(shard[None], (peers, *shard.shape)), axis...  19.3 us
    pallas_call x2, Pallas kernels, partial_exchange(): pl.pallas_call(functools.partial(response_kernel, wide), out_shape=jax.Sh...  18.1 us
    all_to_all x1, blocking collectives, body(): parts = lax.all_to_all(part.reshape(split), BOTH, 0, 0, tiled=True)  14.2 us
    all_to_all x1, waiting for transfers between devices, body(): parts = lax.all_to_all(part.reshape(split), BOTH, 0, 0, tiled=True)  9.68 us
    unnamed x14, local copies, waits for them, and re-layouts  6.47 us
    all_to_all x1, starting transfers between devices, body(): parts = lax.all_to_all(part.reshape(split), BOTH, 0, 0, tiled=True)  4.85 us
    all_to_all x1, starting transfers between devices, sent_to_all(): lax.all_to_all(jnp.broadcast_to(shard[None], (peers, *shard.shape)), axis...  4.78 us
  transfers between devices with their start and end apart: 2, of which 2 were waited for; matrix products, arithmetic and copies ran while one was open for 1% of the time, Pallas kernels for 0%

profile of v1, /device:TPU:1, one launch (start us, length us, event | category | flops | bytes accessed | tf_op | source)
XLA Modules:
  0.0 134.2 jit_solution(14604058713139916986)
XLA Ops:
  0.0 0.0 copy-start.3
  0.0 0.9 broadcast_in_dim.9
  0.9 22.1 %all_to_all.30 = bf16[16,160,128]{2,1,0:T(8,128)(2,1)S(1)} all-to-all(bf16[16,160,128]{2,1,0:T(8,128)(2,1)S(1)} %broadcast_in_dim.9), channel_id=1, replica_groups=mesh['row'=8,'col'=16] {'col'}, dimensions={0} | all-to-all | bytes 1310720 | tf_op jit(solution)/shard_map/all_to_all | solution.py:17
  23.0 0.0 copy-done.3
  23.0 1.2 broadcast_in_dim.8
  24.2 0.0 copy-start.2
  24.2 0.0 copy-start.4
  24.2 0.0 copy-start.5
  24.2 4.8 %all-to-all-start = ((bf16[8,160,512]{2,1,0:T(8,128)(2,1)}), bf16[8,160,512]{2,1,0:T(8,128)(2,1)S(1)}, u32[]{:S(2)}, u32[]{:S(2)}) async-start(bf16[8,160,512]{2,1,0:T(8,128)(2,1)} %broadcast_in_dim.8), calls=%async_computation | async-start | bytes 2621440 | tf_op jit(solution)/shard_map/all_to_all | solution.py:17
  29.0 0.0 copy-done.2
  29.0 0.0 copy-done.4
  29.0 0.0 copy-done.5
  29.0 0.1 divide_convert_fusion.amp_ref
  29.1 0.2 copy.10
  29.4 19.3 %all-to-all-done = bf16[8,160,512]{2,1,0:T(8,128)(2,1)S(1)} async-done(((bf16[8,160,512]{2,1,0:T(8,128)(2,1)}), bf16[8,160,512]{2,1,0:T(8,128)(2,1)S(1)}, u32[]{:S(2)}, u32[]{:S(2)}) %all-to-all-start) | async-done | bytes 1310752 | tf_op jit(solution)/shard_map/all_to_all | solution.py:17
  48.7 0.0 copy-start
  48.7 2.9 %copy-done = bf16[2560,1280]{1,0:T(8,128)(2,1)S(1)} copy-done((bf16[2560,1280]{1,0:T(8,128)(2,1)S(1)}, bf16[2560,1280]{1,0:T(8,128)(2,1)}, u32[]{:S(2)}) %copy-start) | copy-done | bytes 6553624
  51.5 9.1 %shard_map.64 = bf16[128,512]{1,0:T(8,128)(2,1)S(1)} custom-call(bf16[128,512]{1,0:T(8,128)(2,1)S(1)} %divide_convert_fusion.amp_ref, bf16[1280,512]{1,0:T(8,128)(2,1)S(1)} %bitcast.18, bf16[2560,128]{1,0:T(8,128)(2,1)S(1)} %bitcast.21, bf16[128,2560]{1,0:T(8,128)(2,1)S(1)} %bitcast.23, bf16[2560,1280]{1,0:T(8,128)(2,1)S(1)} %copy-done), custom_call_target="tpu_custom_call" | custom-call | tf_op jit(solution)/shard_map/pallas_call | solution.py:63
  60.6 0.7 reshape.57
  61.3 4.8 %all-to-all-start.2 = ((bf16[128,4,128]{2,1,0:T(4,128)(2,1)}), bf16[128,4,128]{2,1,0:T(4,128)(2,1)S(1)}, u32[]{:S(2)}, u32[]{:S(2)}) async-start(bf16[128,4,128]{2,1,0:T(4,128)(2,1)} %reshape.57), calls=%async_computation.2 | async-start | bytes 262144 | tf_op jit(solution)/shard_map/all_to_all | solution.py:98
  66.1 0.6 dynamic_slice.9
  66.7 9.7 %all-to-all-done.2 = bf16[128,4,128]{2,1,0:T(4,128)(2,1)S(1)} async-done(((bf16[128,4,128]{2,1,0:T(4,128)(2,1)}), bf16[128,4,128]{2,1,0:T(4,128)(2,1)S(1)}, u32[]{:S(2)}, u32[]{:S(2)}) %all-to-all-start.2) | async-done | bytes 131104 | tf_op jit(solution)/shard_map/all_to_all | solution.py:98
  76.4 0.1 convert_reduce_fusion.1
  76.6 0.6 fusion
  77.2 14.1 %all_to_all.31 = bf16[128,4,128]{2,1,0:T(4,128)(2,1)S(1)} all-to-all(bf16[128,4,128]{2,1,0:T(4,128)(2,1)S(1)} %broadcast_in_dim.10), channel_id=1, replica_groups=mesh['row'=8,'col'=16] {'row','col'}, dimensions={0} | all-to-all | bytes 262144 | tf_op jit(solution)/shard_map/all_to_all | solution.py:17
  91.4 0.0 copy-start.1
  91.4 2.9 %copy-done.1 = bf16[2560,1280]{1,0:T(8,128)(2,1)S(1)} copy-done((bf16[2560,1280]{1,0:T(8,128)(2,1)S(1)}, bf16[2560,1280]{1,0:T(8,128)(2,1)}, u32[]{:S(2)}) %copy-start.1) | copy-done | bytes 6553624
  94.3 9.1 %shard_map.65 = bf16[128,512]{1,0:T(8,128)(2,1)S(1)} custom-call(bf16[128,512]{1,0:T(8,128)(2,1)S(1)} %bitcast.25, bf16[1280,512]{1,0:T(8,128)(2,1)S(1)} %bitcast.19, bf16[2560,128]{1,0:T(8,128)(2,1)S(1)} %bitcast.22, bf16[128,2560]{1,0:T(8,128)(2,1)S(1)} %bitcast.24, bf16[2560,1280]{1,0:T(8,128)(2,1)S(1)} %copy-done.1), custom_call_target="tpu_custom_call" | custom-call | tf_op jit(solution)/shard_map/pallas_call | solution.py:63
  103.4 14.2 %all_to_all.32 = bf16[128,4,128]{2,1,0:T(4,128)(2,1)S(1)} all-to-all(bf16[128,4,128]{2,1,0:T(4,128)(2,1)S(1)} %reshape.59), channel_id=1, replica_groups=mesh['row'=8,'col'=16] {'row','col'}, dimensions={0} | all-to-all | bytes 262144 | tf_op jit(solution)/shard_map/all_to_all | solution.py:98
  117.5 0.1 convert_reduce_fusion
  117.7 0.6 bitcast_divide_fusion
  118.3 15.2 %all_to_all.33 = f32[128,4,128]{2,1,0:T(4,128)S(1)} all-to-all(f32[128,4,128]{2,1,0:T(4,128)S(1)} %broadcast_in_dim.11), channel_id=1, replica_groups=mesh['row'=8,'col'=16] {'row','col'}, dimensions={0} | all-to-all | bytes 524288 | tf_op jit(solution)/shard_map/all_to_all | solution.py:17
  133.5 0.7 copy.15
  (5 shorter events, 0.1 us)
Async XLA Ops:
  0.0 23.0 %copy-start.3 = (bf16[160,512]{1,0:T(8,128)(2,1)S(1)}, bf16[160,512]{1,0:T(8,128)(2,1)}, u32[]{:S(2)}) copy-start(bf16[160,512]{1,0:T(8,128)(2,1)} %param.8) | copy-start | bytes 491524
  24.2 4.8 %copy-start.2 = (f32[128,512]{1,0:T(8,128)S(1)}, f32[128,512]{1,0:T(8,128)}, u32[]{:S(2)}) copy-start(f32[128,512]{1,0:T(8,128)} %param.9) | copy-start | bytes 786436
  24.2 4.8 %copy-start.4 = (f32[512]{0:T(512)S(1)}, f32[512]{0:T(512)}, u32[]{:S(2)}) copy-start(f32[512]{0:T(512)} %param.11) | copy-start | bytes 6148
  24.2 4.8 %copy-start.5 = (f32[128]{0:T(128)S(1)}, f32[128]{0:T(128)}, u32[]{:S(2)}) copy-start(f32[128]{0:T(128)} %param.10) | copy-start | bytes 1540
  24.2 24.5 %all-to-all-start = ((bf16[8,160,512]{2,1,0:T(8,128)(2,1)}), bf16[8,160,512]{2,1,0:T(8,128)(2,1)S(1)}, u32[]{:S(2)}, u32[]{:S(2)}) async-start(bf16[8,160,512]{2,1,0:T(8,128)(2,1)} %broadcast_in_dim.8), calls=%async_computation | async-start | bytes 2621440 | tf_op jit(solution)/shard_map/all_to_all | solution.py:17
  48.7 2.9 %copy-start = (bf16[2560,1280]{1,0:T(8,128)(2,1)S(1)}, bf16[2560,1280]{1,0:T(8,128)(2,1)}, u32[]{:S(2)}) copy-start(bf16[2560,1280]{1,0:T(8,128)(2,1)} %kern_ref.3) | copy-start | bytes 19660804
  61.3 15.1 %all-to-all-start.2 = ((bf16[128,4,128]{2,1,0:T(4,128)(2,1)}), bf16[128,4,128]{2,1,0:T(4,128)(2,1)S(1)}, u32[]{:S(2)}, u32[]{:S(2)}) async-start(bf16[128,4,128]{2,1,0:T(4,128)(2,1)} %reshape.57), calls=%async_computation.2 | async-start | bytes 262144 | tf_op jit(solution)/shard_map/all_to_all | solution.py:98
  91.4 2.9 %copy-start.1 = (bf16[2560,1280]{1,0:T(8,128)(2,1)S(1)}, bf16[2560,1280]{1,0:T(8,128)(2,1)}, u32[]{:S(2)}) copy-start(bf16[2560,1280]{1,0:T(8,128)(2,1)} %kern_ref.3) | copy-start | bytes 19660804

commit v2 on v1

v2 whole, which is shorter than its diff:
```python
import functools

import jax
import jax.numpy as jnp
from jax import lax
from jax.experimental import pallas as pl
from jax.experimental.pallas import tpu as pltpu
from jax.sharding import PartitionSpec as P


ITERS = 2
LANES = 128
BOTH = ("row", "col")
NT = (((1,), (1,)), ((), ()))


def sent_to_all(shard, axis):
    peers = lax.axis_size(axis)
    return lax.all_to_all(
        jnp.broadcast_to(shard[None], (peers, *shard.shape)), axis, 0, 0, tiled=True
    )


def gathered_by_hops(shard, axis, masks):
    peers = lax.axis_size(axis)
    held, known = shard[None], [0]
    for mask in masks:
        other = lax.ppermute(held, axis, [(i, i ^ mask) for i in range(peers)])
        held = jnp.concatenate([held, other], 0)
        known = known + [k ^ mask for k in known]
    order = [known.index(m) for m in range(peers)]
    assert sorted(known) == list(range(peers))
    return held, order


def gathered_occ(occ):
    held, order = gathered_by_hops(occ, "col", (2, 4, 8, 1))
    mine = lax.axis_index("col")
    placed = pl.pallas_call(
        functools.partial(placed_kernel, order),
        out_shape=jax.ShapeDtypeStruct(held.shape, held.dtype),
        in_specs=[
            pl.BlockSpec(memory_space=pltpu.SMEM),
            pl.BlockSpec(memory_space=pltpu.VMEM),
        ],
        out_specs=pl.BlockSpec(memory_space=pltpu.VMEM),
        compiler_params=pltpu.CompilerParams(vmem_limit_bytes=4 << 20),
    )(mine.reshape(1), held)
    return placed.reshape(-1, occ.shape[1])


def placed_kernel(order, mine_ref, held_ref, out_ref):
    mine = mine_ref[0]
    for m, k in enumerate(order):
        out_ref[jnp.bitwise_xor(mine, m)] = held_ref[k]


def response_kernel(wide, amp_ref, virt_ref, occ_ref, occ_t_ref, kern_ref, out_ref, held_ref, sem):
    f32, b16 = jnp.float32, jnp.bfloat16
    chunks = kern_ref.shape[1] // wide
    copies = [
        pltpu.make_async_copy(
            kern_ref.at[:, pl.ds(chunk * wide, wide)], held_ref.at[chunk], sem.at[chunk]
        )
        for chunk in range(chunks)
    ]
    for copy in copies:
        copy.start()
    total = None
    for chunk, copy in enumerate(copies):
        virt = virt_ref[pl.ds(chunk * wide, wide), :]
        w = lax.dot_general(amp_ref[...], virt, NT, preferred_element_type=f32).astype(b16)
        outer = jnp.dot(occ_ref[...], w, preferred_element_type=f32)
        copy.wait()
        weighted = (held_ref[chunk].astype(f32) * outer).astype(b16)
        contracted = jnp.dot(occ_t_ref[...], weighted, preferred_element_type=f32)
        high = contracted.astype(b16)
        low = (contracted - high.astype(f32)).astype(b16)
        exchange = jnp.dot(high, virt, preferred_element_type=f32)
        exchange += jnp.dot(low, virt, preferred_element_type=f32)
        total = exchange if total is None else total + exchange
    out_ref[...] = total.astype(out_ref.dtype)


def partial_exchange(amp_b, virt_cols, occ_rows, occ_t, kernel):
    rows, cols = kernel.shape
    wide = 256
    vmem = pl.BlockSpec(memory_space=pltpu.VMEM)
    return pl.pallas_call(
        functools.partial(response_kernel, wide),
        out_shape=jax.ShapeDtypeStruct(amp_b.shape, jnp.bfloat16),
        in_specs=[vmem, vmem, vmem, vmem, pl.BlockSpec(memory_space=pltpu.HBM)],
        out_specs=vmem,
        scratch_shapes=[
            pltpu.VMEM((cols // wide, rows, wide), jnp.bfloat16),
            pltpu.SemaphoreType.DMA((cols // wide,)),
        ],
        compiler_params=pltpu.CompilerParams(vmem_limit_bytes=40 << 20),
    )(amp_b, virt_cols, occ_rows, occ_t, pltpu.with_memory_space_constraint(kernel, pltpu.HBM))


def body(kernel, occ, virt, rhs, e_occ, e_virt):
    occupied, virtual = rhs.shape
    split = (occupied, virtual // LANES, LANES)
    mine = lax.axis_index("row") * lax.axis_size("col") + lax.axis_index("col")
    virt_cols = sent_to_all(virt, "row").reshape(-1, virtual)
    occ_rows = gathered_occ(occ)
    occ_t = occ_rows.T
    rhs_mine = lax.dynamic_index_in_dim(rhs, mine, 0, False).reshape(split[1:])
    denom_mine = e_virt.reshape(split[1:]) - lax.dynamic_index_in_dim(e_occ, mine, 0, False)

    amp_b = (rhs / (e_virt[None, :] - e_occ[:, None])).astype(jnp.bfloat16)
    for step in range(ITERS):
        part = partial_exchange(amp_b, virt_cols, occ_rows, occ_t, kernel)
        parts = lax.all_to_all(part.reshape(split), BOTH, 0, 0, tiled=True)
        exchange = jnp.sum(parts.astype(jnp.float32), axis=0)
        amp_mine = (rhs_mine - exchange) / denom_mine
        if step < ITERS - 1:
            amp_b = sent_to_all(amp_mine.astype(jnp.bfloat16), BOTH).reshape(rhs.shape)
    return sent_to_all(amp_mine, BOTH).reshape(rhs.shape)


def solution(mesh):
    in_specs = (P("row", "col"), P(("row", "col"), None), P(("col", "row"), None), P(), P(), P())
    return jax.shard_map(body, mesh=mesh, in_specs=in_specs, out_specs=P(), check_vma=False)
```

time: 135 us -> 115 us (0.85)
  blocking collectives: 65.6 us -> 43.5 us
  starting transfers between devices: 9.62 us -> 22.3 us
  local copies, waits for them, and re-layouts: 10.2 us -> 4.68 us
  waiting for transfers between devices: 29 us -> 25.6 us
    all_to_all x3 -> x2, blocking collectives: 51.4 us -> 29.3 us  [sent_to_all(): lax.all_to_all(jnp.broadcast_to(shard[None], (peers, *shard.shape)), axis...]
    all_to_all x1, waiting for transfers between devices: 19.3 us -> 0.01 us  [sent_to_all(): lax.all_to_all(jnp.broadcast_to(shard[None], (peers, *shard.shape)), axis...]
    ppermute x0 -> x4, waiting for transfers between devices: none -> 16.1 us  [gathered_by_hops(): other = lax.ppermute(held, axis, [(i, i ^ mask) for i in range(peers)])]
    ppermute x0 -> x4, starting transfers between devices: none -> 9.69 us  [gathered_by_hops(): other = lax.ppermute(held, axis, [(i, i ^ mask) for i in range(peers)])]
    unnamed x14, local copies, waits for them, and re-layouts: 6.47 us -> 0.81 us
    all_to_all x1, starting transfers between devices: 4.85 us -> 6.94 us  [body(): parts = lax.all_to_all(part.reshape(split), BOTH, 0, 0, tiled=True)]
  transfers between devices with their start and end apart: 2 -> 6, of which waited for: 2 -> 4; matrix products, arithmetic and copies ran while one was open for 1% -> 3% of each run, Pallas kernels for 0% -> 0%
where the time goes in v2:
time: 115 us
  blocking collectives  43.5 us (38%)
  waiting for transfers between devices  25.6 us (22%)
  starting transfers between devices  22.3 us (19%)
  Pallas kernels  16.9 us (15%)
  local copies, waits for them, and re-layouts  4.68 us (4%)
  other arithmetic  1.85 us (2%)
    all_to_all x2, blocking collectives, sent_to_all(): lax.all_to_all(jnp.broadcast_to(shard[None], (peers, *shard.shape)), axis...  29.3 us
    pallas_call x2, Pallas kernels, partial_exchange(): pl.pallas_call(functools.partial(response_kernel, wide), out_shape=jax.Sh...  16.8 us
    ppermute x4, waiting for transfers between devices, gathered_by_hops(): other = lax.ppermute(held, axis, [(i, i ^ mask) for i in range(peers)])  16.1 us
    all_to_all x1, blocking collectives, body(): parts = lax.all_to_all(part.reshape(split), BOTH, 0, 0, tiled=True)  14.2 us
    ppermute x4, starting transfers between devices, gathered_by_hops(): other = lax.ppermute(held, axis, [(i, i ^ mask) for i in range(peers)])  9.69 us
    all_to_all x1, waiting for transfers between devices, body(): parts = lax.all_to_all(part.reshape(split), BOTH, 0, 0, tiled=True)  9.47 us
    all_to_all x1, starting transfers between devices, body(): parts = lax.all_to_all(part.reshape(split), BOTH, 0, 0, tiled=True)  6.94 us
    all_to_all x1, starting transfers between devices, sent_to_all(): lax.all_to_all(jnp.broadcast_to(shard[None], (peers, *shard.shape)), axis...  5.69 us
  transfers between devices with their start and end apart: 6, of which 4 were waited for; matrix products, arithmetic and copies ran while one was open for 3% of the time, Pallas kernels for 0%

profile of v2, /device:TPU:1, one launch (start us, length us, event | category | flops | bytes accessed | tf_op | source)
XLA Modules:
  0.0 115.0 jit_solution(18355672273760054726)
XLA Ops:
  0.0 2.0 %collective-permute-start = (bf16[1,160,128]{2,1,0:T(8,128)(2,1)}, bf16[1,160,128]{2,1,0:T(8,128)(2,1)S(1)}, u32[]{:S(2)}, u32[]{:S(2)}) collective-permute-start(bf16[1,160,128]{2,1,0:T(8,128)(2,1)} %bitcast.30), channel_id=1, source_target_pairs={{0,2},{1,3},{2,0},{3,1},{4,6},{5,7},{6,4},{7,5},{8,10},{9,11},{10,... | collective-permute-start | bytes 122888 | tf_op jit(solution)/shard_map/ppermute | solution.py:28
  2.0 2.1 %broadcast_in_dim.8 = bf16[8,160,512]{2,1,0:T(8,128)(2,1)} broadcast(bf16[160,512]{1,0:T(8,128)(2,1)} %param.8), dimensions={1,2} | broadcast | bytes 1474560 | tf_op jit(solution)/shard_map/broadcast_in_dim | solution.py:20
  4.1 0.0 copy-start
  4.1 0.0 copy-start.1
  4.1 0.0 copy-start.2
  4.1 0.0 copy-start.3
  4.1 5.7 %all-to-all-start = ((bf16[8,160,512]{2,1,0:T(8,128)(2,1)}), bf16[8,160,512]{2,1,0:T(8,128)(2,1)S(1)}, u32[]{:S(2)}, u32[]{:S(2)}) async-start(bf16[8,160,512]{2,1,0:T(8,128)(2,1)} %broadcast_in_dim.8), calls=%async_computation | async-start | bytes 2621440 | tf_op jit(solution)/shard_map/all_to_all | solution.py:19
  9.8 0.0 collective-permute-done
  9.8 0.0 copy-done
  9.9 2.5 %collective-permute-start.1 = (bf16[2,160,128]{2,1,0:T(8,128)(2,1)S(1)}, bf16[2,160,128]{2,1,0:T(8,128)(2,1)S(1)}, u32[]{:S(2)}, u32[]{:S(2)}) collective-permute-start(bf16[2,160,128]{2,1,0:T(8,128)(2,1)S(1)} %pad_maximum_fusion.2), channel_id=1, source_target_pairs={{0,4},{1,5},{2,6},{3,7},{4,0},{5,1},{6,2},{7,3},{8,12},{9,13},{10,... | collective-permute-start | bytes 245768 | tf_op jit(solution)/shard_map/ppermute | solution.py:28
  12.4 0.0 copy-done.1
  12.4 0.0 copy-done.2
  12.4 0.0 copy-done.3
  12.4 0.1 divide_convert_fusion.amp_ref
  12.5 2.2 %collective-permute-done.1 = bf16[2,160,128]{2,1,0:T(8,128)(2,1)S(1)} collective-permute-done((bf16[2,160,128]{2,1,0:T(8,128)(2,1)S(1)}, bf16[2,160,128]{2,1,0:T(8,128)(2,1)S(1)}, u32[]{:S(2)}, u32[]{:S(2)}) %collective-permute-start.1) | collective-permute-done | bytes 81952 | tf_op jit(solution)/shard_map/ppermute | solution.py:28
  14.8 3.4 %collective-permute-start.2 = (bf16[4,160,128]{2,1,0:T(8,128)(2,1)S(1)}, bf16[4,160,128]{2,1,0:T(8,128)(2,1)S(1)}, u32[]{:S(2)}, u32[]{:S(2)}) collective-permute-start(bf16[4,160,128]{2,1,0:T(8,128)(2,1)S(1)} %pad_maximum_fusion.1), channel_id=1, source_target_pairs={{0,8},{1,9},{2,10},{3,11},{4,12},{5,13},{6,14},{7,15},{8,0},{9,1},... | collective-permute-start | bytes 491528 | tf_op jit(solution)/shard_map/ppermute | solution.py:28
  18.2 12.7 %collective-permute-done.2 = bf16[4,160,128]{2,1,0:T(8,128)(2,1)S(1)} collective-permute-done((bf16[4,160,128]{2,1,0:T(8,128)(2,1)S(1)}, bf16[4,160,128]{2,1,0:T(8,128)(2,1)S(1)}, u32[]{:S(2)}, u32[]{:S(2)}) %collective-permute-start.2) | collective-permute-done | bytes 163872 | tf_op jit(solution)/shard_map/ppermute | solution.py:28
  30.9 1.8 %collective-permute-start.3 = (bf16[8,160,128]{2,1,0:T(8,128)(2,1)S(1)}, bf16[8,160,128]{2,1,0:T(8,128)(2,1)S(1)}, u32[]{:S(2)}, u32[]{:S(2)}) collective-permute-start(bf16[8,160,128]{2,1,0:T(8,128)(2,1)S(1)} %pad_maximum_fusion), channel_id=1, source_target_pairs={{0,1},{1,0},{2,3},{3,2},{4,5},{5,4},{6,7},{7,6},{8,9},{9,8},{10,11... | collective-permute-start | bytes 983048 | tf_op jit(solution)/shard_map/ppermute | solution.py:28
  32.7 1.2 %collective-permute-done.3 = bf16[8,160,128]{2,1,0:T(8,128)(2,1)S(1)} collective-permute-done((bf16[8,160,128]{2,1,0:T(8,128)(2,1)S(1)}, bf16[8,160,128]{2,1,0:T(8,128)(2,1)S(1)}, u32[]{:S(2)}, u32[]{:S(2)}) %collective-permute-start.3) | collective-permute-done | bytes 327712 | tf_op jit(solution)/shard_map/ppermute | solution.py:28
  34.0 0.1 shard_map.64
  34.0 0.2 copy.10
  34.3 0.0 all-to-all-done
  34.3 8.4 %shard_map.65 = bf16[128,512]{1,0:T(8,128)(2,1)S(1)} custom-call(bf16[128,512]{1,0:T(8,128)(2,1)S(1)} %divide_convert_fusion.amp_ref, bf16[1280,512]{1,0:T(8,128)(2,1)S(1)} %bitcast.21, bf16[2560,128]{1,0:T(8,128)(2,1)S(1)} %bitcast.24, bf16[128,2560]{1,0:T(8,128)(2,1)S(1)} %bitcast.26, bf16[2560,1280]{1,0:T(8,128)(2,1)} %kern_ref.3), custom_call_target="tpu_custom_call" | custom-call | tf_op jit(solution)/shard_map/pallas_call | solution.py:89
  42.7 0.7 reshape.60
  43.4 6.9 %all-to-all-start.1 = ((bf16[128,4,128]{2,1,0:T(4,128)(2,1)}), bf16[128,4,128]{2,1,0:T(4,128)(2,1)S(1)}, u32[]{:S(2)}, u32[]{:S(2)}) async-start(bf16[128,4,128]{2,1,0:T(4,128)(2,1)} %reshape.60), calls=%async_computation.1 | async-start | bytes 262144 | tf_op jit(solution)/shard_map/all_to_all | solution.py:115
  50.4 0.7 dynamic_slice.9
  51.0 9.5 %all-to-all-done.1 = bf16[128,4,128]{2,1,0:T(4,128)(2,1)S(1)} async-done(((bf16[128,4,128]{2,1,0:T(4,128)(2,1)}), bf16[128,4,128]{2,1,0:T(4,128)(2,1)S(1)}, u32[]{:S(2)}, u32[]{:S(2)}) %all-to-all-start.1) | async-done | bytes 131104 | tf_op jit(solution)/shard_map/all_to_all | solution.py:115
  60.5 0.1 convert_reduce_fusion.1
  60.6 0.7 fusion
  61.4 14.1 %all_to_all.25 = bf16[128,4,128]{2,1,0:T(4,128)(2,1)S(1)} all-to-all(bf16[128,4,128]{2,1,0:T(4,128)(2,1)S(1)} %broadcast_in_dim.10), channel_id=1, replica_groups=mesh['row'=8,'col'=16] {'row','col'}, dimensions={0} | all-to-all | bytes 262144 | tf_op jit(solution)/shard_map/all_to_all | solution.py:19
  75.6 8.4 %shard_map.66 = bf16[128,512]{1,0:T(8,128)(2,1)S(1)} custom-call(bf16[128,512]{1,0:T(8,128)(2,1)S(1)} %bitcast.28, bf16[1280,512]{1,0:T(8,128)(2,1)S(1)} %bitcast.22, bf16[2560,128]{1,0:T(8,128)(2,1)S(1)} %bitcast.25, bf16[128,2560]{1,0:T(8,128)(2,1)S(1)} %bitcast.27, bf16[2560,1280]{1,0:T(8,128)(2,1)} %kern_ref.3), custom_call_target="tpu_custom_call" | custom-call | tf_op jit(solution)/shard_map/pallas_call | solution.py:89
  84.0 14.2 %all_to_all.26 = bf16[128,4,128]{2,1,0:T(4,128)(2,1)S(1)} all-to-all(bf16[128,4,128]{2,1,0:T(4,128)(2,1)S(1)} %reshape.62), channel_id=1, replica_groups=mesh['row'=8,'col'=16] {'row','col'}, dimensions={0} | all-to-all | bytes 262144 | tf_op jit(solution)/shard_map/all_to_all | solution.py:115
  98.2 0.1 convert_reduce_fusion
  98.3 0.7 bitcast_divide_fusion
  99.1 15.2 %all_to_all.27 = f32[128,4,128]{2,1,0:T(4,128)S(1)} all-to-all(f32[128,4,128]{2,1,0:T(4,128)S(1)} %broadcast_in_dim.11), channel_id=1, replica_groups=mesh['row'=8,'col'=16] {'row','col'}, dimensions={0} | all-to-all | bytes 524288 | tf_op jit(solution)/shard_map/all_to_all | solution.py:19
  114.3 0.7 copy.15
  (13 shorter events, 0.3 us)
Async XLA Ops:
  0.0 9.8 %collective-permute-start = (bf16[1,160,128]{2,1,0:T(8,128)(2,1)}, bf16[1,160,128]{2,1,0:T(8,128)(2,1)S(1)}, u32[]{:S(2)}, u32[]{:S(2)}) collective-permute-start(bf16[1,160,128]{2,1,0:T(8,128)(2,1)} %bitcast.30), channel_id=1, source_target_pairs={{0,2},{1,3},{2,0},{3,1},{4,6},{5,7},{6,4},{7,5},{8,10},{9,11},{10,... | collective-permute-start | bytes 122888 | tf_op jit(solution)/shard_map/ppermute | solution.py:28
  4.1 5.7 %copy-start = (bf16[160,128]{1,0:T(8,128)(2,1)S(1)}, bf16[160,128]{1,0:T(8,128)(2,1)}, u32[]{:S(2)}) copy-start(bf16[160,128]{1,0:T(8,128)(2,1)} %param.7) | copy-start | bytes 122884
  4.1 8.3 %copy-start.1 = (f32[128,512]{1,0:T(8,128)S(1)}, f32[128,512]{1,0:T(8,128)}, u32[]{:S(2)}) copy-start(f32[128,512]{1,0:T(8,128)} %param.9) | copy-start | bytes 786436
  4.1 8.3 %copy-start.2 = (f32[512]{0:T(512)S(1)}, f32[512]{0:T(512)}, u32[]{:S(2)}) copy-start(f32[512]{0:T(512)} %param.11) | copy-start | bytes 6148
  4.1 8.3 %copy-start.3 = (f32[128]{0:T(128)S(1)}, f32[128]{0:T(128)}, u32[]{:S(2)}) copy-start(f32[128]{0:T(128)} %param.10) | copy-start | bytes 1540
  4.1 30.1 %all-to-all-start = ((bf16[8,160,512]{2,1,0:T(8,128)(2,1)}), bf16[8,160,512]{2,1,0:T(8,128)(2,1)S(1)}, u32[]{:S(2)}, u32[]{:S(2)}) async-start(bf16[8,160,512]{2,1,0:T(8,128)(2,1)} %broadcast_in_dim.8), calls=%async_computation | async-start | bytes 2621440 | tf_op jit(solution)/shard_map/all_to_all | solution.py:19
  9.9 4.9 %collective-permute-start.1 = (bf16[2,160,128]{2,1,0:T(8,128)(2,1)S(1)}, bf16[2,160,128]{2,1,0:T(8,128)(2,1)S(1)}, u32[]{:S(2)}, u32[]{:S(2)}) collective-permute-start(bf16[2,160,128]{2,1,0:T(8,128)(2,1)S(1)} %pad_maximum_fusion.2), channel_id=1, source_target_pairs={{0,4},{1,5},{2,6},{3,7},{4,0},{5,1},{6,2},{7,3},{8,12},{9,13},{10,... | collective-permute-start | bytes 245768 | tf_op jit(solution)/shard_map/ppermute | solution.py:28
  14.8 16.1 %collective-permute-start.2 = (bf16[4,160,128]{2,1,0:T(8,128)(2,1)S(1)}, bf16[4,160,128]{2,1,0:T(8,128)(2,1)S(1)}, u32[]{:S(2)}, u32[]{:S(2)}) collective-permute-start(bf16[4,160,128]{2,1,0:T(8,128)(2,1)S(1)} %pad_maximum_fusion.1), channel_id=1, source_target_pairs={{0,8},{1,9},{2,10},{3,11},{4,12},{5,13},{6,14},{7,15},{8,0},{9,1},... | collective-permute-start | bytes 491528 | tf_op jit(solution)/shard_map/ppermute | solution.py:28
  30.9 3.0 %collective-permute-start.3 = (bf16[8,160,128]{2,1,0:T(8,128)(2,1)S(1)}, bf16[8,160,128]{2,1,0:T(8,128)(2,1)S(1)}, u32[]{:S(2)}, u32[]{:S(2)}) collective-permute-start(bf16[8,160,128]{2,1,0:T(8,128)(2,1)S(1)} %pad_maximum_fusion), channel_id=1, source_target_pairs={{0,1},{1,0},{2,3},{3,2},{4,5},{5,4},{6,7},{7,6},{8,9},{9,8},{10,11... | collective-permute-start | bytes 983048 | tf_op jit(solution)/shard_map/ppermute | solution.py:28
  43.4 17.1 %all-to-all-start.1 = ((bf16[128,4,128]{2,1,0:T(4,128)(2,1)}), bf16[128,4,128]{2,1,0:T(4,128)(2,1)S(1)}, u32[]{:S(2)}, u32[]{:S(2)}) async-start(bf16[128,4,128]{2,1,0:T(4,128)(2,1)} %reshape.60), calls=%async_computation.1 | async-start | bytes 262144 | tf_op jit(solution)/shard_map/all_to_all | solution.py:115

commit v3 on v0

v3 whole, which is shorter than its diff:
```python
import functools

import jax
import jax.numpy as jnp
from jax import lax
from jax.experimental import pallas as pl
from jax.experimental.pallas import tpu as pltpu
from jax.sharding import PartitionSpec as P


ITERS = 2
LANES = 128
BOTH = ("row", "col")
NT = (((1,), (1,)), ((), ()))
TN = (((0,), (0,)), ((), ()))
VMEM = pl.BlockSpec(memory_space=pltpu.VMEM)
SMEM = pl.BlockSpec(memory_space=pltpu.SMEM)
HBM = pl.BlockSpec(memory_space=pltpu.HBM)


def sent_to_all(shard, axis):
    peers = lax.axis_size(axis)
    return lax.all_to_all(
        jnp.broadcast_to(shard[None], (peers, *shard.shape)), axis, 0, 0, tiled=True
    )


def place_kernel(axis, order, held_ref, out_ref):
    mine, tall = lax.axis_index(axis), held_ref.shape[1]
    for m, k in enumerate(order):
        start = pl.multiple_of(jnp.bitwise_xor(mine, m) * tall, tall)
        out_ref[pl.ds(start, tall), :] = held_ref[k]


def gathered_by_hops(shard, axis, masks):
    peers = lax.axis_size(axis)
    held, known = shard[None], [0]
    for mask in masks:
        other = lax.ppermute(held, axis, [(i, i ^ mask) for i in range(peers)])
        held = jnp.concatenate([held, other], 0)
        known = known + [k ^ mask for k in known]
    order = [known.index(m) for m in range(peers)]
    return pl.pallas_call(
        functools.partial(place_kernel, axis, order),
        out_shape=jax.ShapeDtypeStruct((peers * shard.shape[0], shard.shape[1]), shard.dtype),
        in_specs=[VMEM],
        out_specs=VMEM,
        compiler_params=pltpu.CompilerParams(vmem_limit_bytes=4 << 20),
    )(held)


def own_kernel(e_occ_ref, rhs_ref, e_virt_ref, rhs_mine_ref, denom_ref):
    tall, lanes = denom_ref.shape
    mine = lax.axis_index("row") * lax.axis_size("col") + lax.axis_index("col")
    group, part = mine // e_virt_ref.shape[0], mine % e_virt_ref.shape[0]
    pair = rhs_ref[
        pl.ds(pl.multiple_of(group // 2 * (2 * tall), 2 * tall), 2 * tall),
        pl.ds(pl.multiple_of(part * lanes, lanes), lanes),
    ]
    rhs_mine_ref[...] = jnp.where(group % 2 == 0, pair[:tall], pair[tall:])
    for row in range(tall):
        denom_ref[pl.ds(row, 1), :] = e_virt_ref[pl.ds(part, 1), :] - e_occ_ref[group * tall + row]


def own_block(rhs, e_occ, e_virt, tall):
    small = jax.ShapeDtypeStruct((tall, LANES), jnp.float32)
    return pl.pallas_call(
        own_kernel,
        out_shape=(small, small),
        in_specs=[SMEM, VMEM, VMEM],
        out_specs=(VMEM, VMEM),
        compiler_params=pltpu.CompilerParams(vmem_limit_bytes=1 << 20),
    )(e_occ, rhs, e_virt.reshape(-1, LANES))


def put_together(blocks_ref, out_ref):
    count, tall, lanes = blocks_ref.shape
    parts = out_ref.shape[1] // lanes
    for block in range(count):
        row, column = block // parts * tall, block % parts * lanes
        out_ref[row : row + tall, column : column + lanes] = blocks_ref[block]


def whole(blocks, shape):
    return pl.pallas_call(
        put_together,
        out_shape=jax.ShapeDtypeStruct(shape, blocks.dtype),
        in_specs=[VMEM],
        compiler_params=pltpu.CompilerParams(vmem_limit_bytes=4 << 20),
    )(blocks)


def response_kernel(cuts, tall, amp_ref, virt_ref, occ_ref, kern_ref, out_ref, *held):
    f32, b16 = jnp.float32, jnp.bfloat16
    if len(amp_ref.shape) == 3:
        *held, joined_ref = held
        put_together(amp_ref, joined_ref)
        amp_ref = joined_ref
    blocks = occ_ref.shape[0] // tall
    waits = {}
    if cuts:
        held_ref, sem = held
        for i, (first, last) in enumerate(zip(cuts, (*cuts[1:], blocks))):
            part = pl.ds(first * tall, (last - first) * tall)
            waits[first] = pltpu.make_async_copy(kern_ref.at[part], held_ref.at[part], sem.at[i])
            waits[first].start()
        kern_ref = held_ref
    w = lax.dot_general(amp_ref[...], virt_ref[...], NT, preferred_element_type=f32).astype(b16)

    def outer_of(block):
        return jnp.dot(occ_ref[pl.ds(block * tall, tall), :], w, preferred_element_type=f32)

    ahead, contracted = outer_of(0), None
    for block in range(blocks):
        here = pl.ds(block * tall, tall)
        if block in waits:
            waits[block].wait()
        outer = ahead
        if block + 1 < blocks:
            ahead = outer_of(block + 1)
        weighted = (kern_ref[here, :].astype(f32) * outer).astype(b16)
        more = lax.dot_general(occ_ref[here, :], weighted, TN, preferred_element_type=f32)
        contracted = more if contracted is None else contracted + more
    high = contracted.astype(b16)
    low = (contracted - high.astype(f32)).astype(b16)
    exchange = jnp.dot(high, virt_ref[...], preferred_element_type=f32)
    exchange += jnp.dot(low, virt_ref[...], preferred_element_type=f32)
    _, rows, lanes = out_ref.shape
    parts = exchange.shape[1] // lanes
    for group in range(exchange.shape[0] // rows):
        for part in range(parts):
            out_ref[group * parts + part] = exchange[
                group * rows : (group + 1) * rows, part * lanes : (part + 1) * lanes
            ].astype(out_ref.dtype)


def partial_exchange(amp_b, virt_cols, occ_rows, kernel, pieces, cuts=()):
    out = jax.ShapeDtypeStruct(pieces, jnp.bfloat16)
    held = jax.ShapeDtypeStruct(kernel.shape, kernel.dtype)
    return pl.pallas_call(
        functools.partial(response_kernel, cuts, 512),
        out_shape=(out, held) if cuts else out,
        in_specs=[VMEM, VMEM, VMEM, HBM if cuts else VMEM],
        out_specs=(VMEM, VMEM) if cuts else VMEM,
        scratch_shapes=[pltpu.SemaphoreType.DMA((len(cuts),))]
        if cuts
        else [pltpu.VMEM((occ_rows.shape[1], virt_cols.shape[1]), jnp.bfloat16)],
        compiler_params=pltpu.CompilerParams(vmem_limit_bytes=40 << 20),
    )(amp_b, virt_cols, occ_rows, kernel)


def body(kernel, occ, virt, rhs, e_occ, e_virt):
    occupied, virtual = rhs.shape
    devices = lax.axis_size(BOTH)
    pieces = (devices, occupied * virtual // (devices * LANES), LANES)
    virt_cols = sent_to_all(virt, "row").reshape(-1, virtual)
    occ_rows = gathered_by_hops(occ, "col", (8, 4, 2, 1))
    rhs_mine, denom_mine = own_block(rhs, e_occ, e_virt, pieces[1])

    amp_b = (rhs / (e_virt[None, :] - e_occ[:, None])).astype(jnp.bfloat16)
    kernel = pltpu.with_memory_space_constraint(kernel, pltpu.HBM)
    for step in range(ITERS):
        if step == 0:
            part, kernel = partial_exchange(amp_b, virt_cols, occ_rows, kernel, pieces, (0, 2))
        else:
            part = partial_exchange(amp_b, virt_cols, occ_rows, kernel, pieces)
        parts = lax.all_to_all(part, BOTH, 0, 0, tiled=True)
        exchange = jnp.sum(parts.astype(jnp.float32), axis=0)
        amp_mine = (rhs_mine - exchange) / denom_mine
        if step < ITERS - 1:
            amp_b = sent_to_all(amp_mine.astype(jnp.bfloat16), BOTH)
    return whole(sent_to_all(amp_mine, BOTH), rhs.shape)


def solution(mesh):
    in_specs = (P("row", "col"), P(("row", "col"), None), P(("col", "row"), None), P(), P(), P())
    return jax.shard_map(body, mesh=mesh, in_specs=in_specs, out_specs=P(), check_vma=False)
```

time: 372 us -> 106 us (0.28)
  waiting for transfers between devices: 281 us -> 16.5 us
  matrix products: 37.4 us -> 0 us
  starting transfers between devices: 6.44 us -> 22.7 us
  blocking collectives: 28.9 us -> 43.5 us
  between operations: 13.5 us -> 0.15 us
  Pallas kernels: 0 us -> 10.4 us
  local copies, waits for them, and re-layouts: 2.15 us -> 8.66 us
    psum x2 -> x0, waiting for transfers between devices: 281 us -> none  [body(): exchange = lax.psum(projection, ('row', 'col'))]
    all_to_all x0 -> x3, blocking collectives: none -> 43.5 us  [the longest x2 29.3 us: sent_to_all(): lax.all_to_all(jnp.broadcast_to(shard[None], (peers, *shard.shape)), axis...]
    dot_general x14 -> x0, matrix products: 37.4 us -> none  [the longest x10 28.8 us: fold(): lax.dot_general(occ_piece, weighted, (((0,), (0,)), ((), ())), preferred_...]
    all_gather x1 -> x0, blocking collectives: 28.9 us -> none  [body(): occ_full = lax.all_gather(occ, 'col', axis=0, tiled=True)]
    ppermute x0 -> x4, starting transfers between devices: none -> 11.8 us  [gathered_by_hops(): other = lax.ppermute(held, axis, [(i, i ^ mask) for i in range(peers)])]
    pallas_call x0 -> x5, Pallas kernels: none -> 10.4 us  [the longest x2 9.04 us: partial_exchange(): pl.pallas_call(functools.partial(response_kernel, cuts, 512), out_shape=(...]
    all_to_all x0 -> x1, waiting for transfers between devices: none -> 9.54 us  [body(): parts = lax.all_to_all(part, BOTH, 0, 0, tiled=True)]
    unnamed x8 -> x14, local copies, waits for them, and re-layouts: 0.01 us -> 6.43 us
  transfers between devices with their start and end apart: 3 -> 6, of which waited for: 2 -> 5; matrix products, arithmetic and copies ran while one was open for 1% -> 6% of each run, Pallas kernels for 0% -> 1%
where the time goes in v3:
time: 106 us
  blocking collectives  43.5 us (41%)
  starting transfers between devices  22.7 us (21%)
  waiting for transfers between devices  16.5 us (16%)
  Pallas kernels  10.4 us (10%)
  local copies, waits for them, and re-layouts  8.66 us (8%)
  other arithmetic  3.81 us (4%)
    all_to_all x2, blocking collectives, sent_to_all(): lax.all_to_all(jnp.broadcast_to(shard[None], (peers, *shard.shape)), axis...  29.3 us
    all_to_all x1, blocking collectives, body(): parts = lax.all_to_all(part, BOTH, 0, 0, tiled=True)  14.2 us
    ppermute x4, starting transfers between devices, gathered_by_hops(): other = lax.ppermute(held, axis, [(i, i ^ mask) for i in range(peers)])  11.8 us
    all_to_all x1, waiting for transfers between devices, body(): parts = lax.all_to_all(part, BOTH, 0, 0, tiled=True)  9.54 us
    pallas_call x2, Pallas kernels, partial_exchange(): pl.pallas_call(functools.partial(response_kernel, cuts, 512), out_shape=(...  9.04 us
    unnamed x14, local copies, waits for them, and re-layouts  6.43 us
    all_to_all x1, starting transfers between devices, body(): parts = lax.all_to_all(part, BOTH, 0, 0, tiled=True)  6.18 us
    all_to_all x1, starting transfers between devices, sent_to_all(): lax.all_to_all(jnp.broadcast_to(shard[None], (peers, *shard.shape)), axis...  4.65 us
  transfers between devices with their start and end apart: 6, of which 5 were waited for; matrix products, arithmetic and copies ran while one was open for 6% of the time, Pallas kernels for 1%

profile of v3, /device:TPU:1, one launch (start us, length us, event | category | flops | bytes accessed | tf_op | source)
XLA Modules:
  0.0 105.7 jit_solution(17978861000759394115)
XLA Ops:
  0.0 4.4 %collective-permute-start = (bf16[1,160,128]{2,1,0:T(8,128)(2,1)}, bf16[1,160,128]{2,1,0:T(8,128)(2,1)S(1)}, u32[]{:S(2)}, u32[]{:S(2)}) collective-permute-start(bf16[1,160,128]{2,1,0:T(8,128)(2,1)} %bitcast.7), channel_id=1, source_target_pairs={{0,8},{1,9},{2,10},{3,11},{4,12},{5,13},{6,14},{7,15},{8,0},{9,1},... | collective-permute-start | bytes 122888 | tf_op jit(solution)/shard_map/ppermute | solution.py:39
  4.4 2.1 %broadcast_in_dim.8 = bf16[8,160,512]{2,1,0:T(8,128)(2,1)} broadcast(bf16[160,512]{1,0:T(8,128)(2,1)} %param.8), dimensions={1,2} | broadcast | bytes 1474560 | tf_op jit(solution)/shard_map/broadcast_in_dim | solution.py:24
  6.5 4.6 %all-to-all-start = ((bf16[8,160,512]{2,1,0:T(8,128)(2,1)}), bf16[8,160,512]{2,1,0:T(8,128)(2,1)S(1)}, u32[]{:S(2)}, u32[]{:S(2)}) async-start(bf16[8,160,512]{2,1,0:T(8,128)(2,1)} %broadcast_in_dim.8), calls=%async_computation | async-start | bytes 2621440 | tf_op jit(solution)/shard_map/all_to_all | solution.py:23
  11.2 0.0 copy-start.2
  11.2 0.0 copy-start.3
  11.2 0.0 copy-start.4
  11.2 0.0 collective-permute-done
  11.2 0.8 pad_maximum_fusion.2
  12.0 2.8 %collective-permute-start.1 = (bf16[2,160,128]{2,1,0:T(8,128)(2,1)S(1)}, bf16[2,160,128]{2,1,0:T(8,128)(2,1)S(1)}, u32[]{:S(2)}, u32[]{:S(2)}) collective-permute-start(bf16[2,160,128]{2,1,0:T(8,128)(2,1)S(1)} %pad_maximum_fusion.2), channel_id=1, source_target_pairs={{0,4},{1,5},{2,6},{3,7},{4,0},{5,1},{6,2},{7,3},{8,12},{9,13},{10,... | collective-permute-start | bytes 245768 | tf_op jit(solution)/shard_map/ppermute | solution.py:39
  14.9 1.1 %divide_convert_fusion.amp_ref = bf16[128,512]{1,0:T(8,128)(2,1)S(1)} fusion(f32[128,512]{1,0:T(8,128)} %rhs_ref.1, f32[128]{0:T(128)} %e_occ_ref.1, f32[512]{0:T(512)} %param.11), kind=kLoop, calls=%fused_computation.3 | loop fusion | flops 196608 | bytes 395776 | tf_op jit(solution)/shard_map/convert_element_type | solution.py:160
  15.9 1.0 collective-permute-done.1
  16.9 0.8 pad_maximum_fusion.1
  17.7 1.3 %collective-permute-start.2 = (bf16[4,160,128]{2,1,0:T(8,128)(2,1)S(1)}, bf16[4,160,128]{2,1,0:T(8,128)(2,1)S(1)}, u32[]{:S(2)}, u32[]{:S(2)}) collective-permute-start(bf16[4,160,128]{2,1,0:T(8,128)(2,1)S(1)} %pad_maximum_fusion.1), channel_id=1, source_target_pairs={{0,2},{1,3},{2,0},{3,1},{4,6},{5,7},{6,4},{7,5},{8,10},{9,11},{10,... | collective-permute-start | bytes 491528 | tf_op jit(solution)/shard_map/ppermute | solution.py:39
  19.0 0.8 constant_dynamic-update-slice_fusion.4
  19.8 2.5 %collective-permute-done.2 = bf16[4,160,128]{2,1,0:T(8,128)(2,1)S(1)} collective-permute-done((bf16[4,160,128]{2,1,0:T(8,128)(2,1)S(1)}, bf16[4,160,128]{2,1,0:T(8,128)(2,1)S(1)}, u32[]{:S(2)}, u32[]{:S(2)}) %collective-permute-start.2) | collective-permute-done | bytes 163872 | tf_op jit(solution)/shard_map/ppermute | solution.py:39
  22.2 0.8 pad_maximum_fusion
  23.1 3.3 %collective-permute-start.3 = (bf16[8,160,128]{2,1,0:T(8,128)(2,1)S(1)}, bf16[8,160,128]{2,1,0:T(8,128)(2,1)S(1)}, u32[]{:S(2)}, u32[]{:S(2)}) collective-permute-start(bf16[8,160,128]{2,1,0:T(8,128)(2,1)S(1)} %pad_maximum_fusion), channel_id=1, source_target_pairs={{0,1},{1,0},{2,3},{3,2},{4,5},{5,4},{6,7},{7,6},{8,9},{9,8},{10,11... | collective-permute-start | bytes 983048 | tf_op jit(solution)/shard_map/ppermute | solution.py:39
  26.4 1.2 %collective-permute-done.3 = bf16[8,160,128]{2,1,0:T(8,128)(2,1)S(1)} collective-permute-done((bf16[8,160,128]{2,1,0:T(8,128)(2,1)S(1)}, bf16[8,160,128]{2,1,0:T(8,128)(2,1)S(1)}, u32[]{:S(2)}, u32[]{:S(2)}) %collective-permute-start.3) | collective-permute-done | bytes 327712 | tf_op jit(solution)/shard_map/ppermute | solution.py:39
  27.7 0.1 shard_map.65.occ_ref
  27.8 2.3 %all-to-all-done = bf16[8,160,512]{2,1,0:T(8,128)(2,1)S(1)} async-done(((bf16[8,160,512]{2,1,0:T(8,128)(2,1)}), bf16[8,160,512]{2,1,0:T(8,128)(2,1)S(1)}, u32[]{:S(2)}, u32[]{:S(2)}) %all-to-all-start) | async-done | bytes 1310752 | tf_op jit(solution)/shard_map/all_to_all | solution.py:23
  30.1 5.5 %shard_map.66 = (bf16[128,4,128]{2,1,0:T(4,128)(2,1)}, bf16[2560,1280]{1,0:T(8,128)(2,1)S(1)}) custom-call(bf16[128,512]{1,0:T(8,128)(2,1)S(1)} %divide_convert_fusion.amp_ref, bf16[1280,512]{1,0:T(8,128)(2,1)S(1)} %bitcast.4, bf16[2560,128]{1,0:T(8,128)(2,1)S(1)} %shard_map.65.occ_ref, bf16[2560,1280]{1,0:T(8,128)(2,1)} %kern_ref.1), custom_call_target="tpu_custom_call" | custom-call | tf_op jit(solution)/shard_map/pallas_call | solution.py:140
  35.6 0.0 copy-start
  35.6 2.7 %copy-done = bf16[2560,1280]{1,0:T(8,128)(2,1)} copy-done((bf16[2560,1280]{1,0:T(8,128)(2,1)}, bf16[2560,1280]{1,0:T(8,128)(2,1)S(1)}, u32[]{:S(2)}) %copy-start) | copy-done | bytes 6553624
  38.4 6.2 %all-to-all-start.1 = ((bf16[128,4,128]{2,1,0:T(4,128)(2,1)}), bf16[128,4,128]{2,1,0:T(4,128)(2,1)S(1)}, u32[]{:S(2)}, u32[]{:S(2)}) async-start(bf16[128,4,128]{2,1,0:T(4,128)(2,1)} %get-tuple-element.10), calls=%async_computation.1 | async-start | bytes 262144 | tf_op jit(solution)/shard_map/all_to_all | solution.py:167
  44.5 0.0 copy-done.2
  44.5 0.0 copy-done.3
  44.6 0.0 copy-done.4
  44.6 0.6 shard_map.64
  45.1 9.5 %all-to-all-done.1 = bf16[128,4,128]{2,1,0:T(4,128)(2,1)S(1)} async-done(((bf16[128,4,128]{2,1,0:T(4,128)(2,1)}), bf16[128,4,128]{2,1,0:T(4,128)(2,1)S(1)}, u32[]{:S(2)}, u32[]{:S(2)}) %all-to-all-start.1) | async-done | bytes 131104 | tf_op jit(solution)/shard_map/all_to_all | solution.py:167
  54.7 0.1 convert_reduce_fusion.1
  54.9 14.1 %all_to_all.25.amp_ref = bf16[128,4,128]{2,1,0:T(4,128)(2,1)S(1)} all-to-all(bf16[128,4,128]{2,1,0:T(4,128)(2,1)S(1)} %broadcast_in_dim.10), channel_id=1, replica_groups=mesh['row'=8,'col'=16] {'row','col'}, dimensions={0} | all-to-all | bytes 262144 | tf_op jit(solution)/shard_map/all_to_all | solution.py:23
  69.0 0.0 copy-start.1
  69.0 2.9 %copy-done.1 = bf16[2560,1280]{1,0:T(8,128)(2,1)S(1)} copy-done((bf16[2560,1280]{1,0:T(8,128)(2,1)S(1)}, bf16[2560,1280]{1,0:T(8,128)(2,1)}, u32[]{:S(2)}) %copy-start.1) | copy-done | bytes 6553624
  71.9 3.5 %shard_map.67 = bf16[128,4,128]{2,1,0:T(4,128)(2,1)S(1)} custom-call(bf16[128,4,128]{2,1,0:T(4,128)(2,1)S(1)} %all_to_all.25.amp_ref, bf16[1280,512]{1,0:T(8,128)(2,1)S(1)} %bitcast.5, bf16[2560,128]{1,0:T(8,128)(2,1)S(1)} %shard_map.65.occ_ref, bf16[2560,1280]{1,0:T(8,128)(2,1)S(1)} %copy-done.1), custom_call_target="tpu_custom_call" | custom-call | tf_op jit(solution)/shard_map/pallas_call | solution.py:140
  75.4 14.2 %all_to_all.26 = bf16[128,4,128]{2,1,0:T(4,128)(2,1)S(1)} all-to-all(bf16[128,4,128]{2,1,0:T(4,128)(2,1)S(1)} %shard_map.67), channel_id=1, replica_groups=mesh['row'=8,'col'=16] {'row','col'}, dimensions={0} | all-to-all | bytes 262144 | tf_op jit(solution)/shard_map/all_to_all | solution.py:167
  89.6 0.1 convert_reduce_fusion
  89.8 15.2 %all_to_all.27.blocks_ref = f32[128,4,128]{2,1,0:T(4,128)S(1)} all-to-all(f32[128,4,128]{2,1,0:T(4,128)S(1)} %broadcast_in_dim.11), channel_id=1, replica_groups=mesh['row'=8,'col'=16] {'row','col'}, dimensions={0} | all-to-all | bytes 524288 | tf_op jit(solution)/shard_map/all_to_all | solution.py:23
  104.9 0.8 shard_map.68
  (8 shorter events, 0.2 us)
Async XLA Ops:
  0.0 11.2 %collective-permute-start = (bf16[1,160,128]{2,1,0:T(8,128)(2,1)}, bf16[1,160,128]{2,1,0:T(8,128)(2,1)S(1)}, u32[]{:S(2)}, u32[]{:S(2)}) collective-permute-start(bf16[1,160,128]{2,1,0:T(8,128)(2,1)} %bitcast.7), channel_id=1, source_target_pairs={{0,8},{1,9},{2,10},{3,11},{4,12},{5,13},{6,14},{7,15},{8,0},{9,1},... | collective-permute-start | bytes 122888 | tf_op jit(solution)/shard_map/ppermute | solution.py:39
  6.5 23.6 %all-to-all-start = ((bf16[8,160,512]{2,1,0:T(8,128)(2,1)}), bf16[8,160,512]{2,1,0:T(8,128)(2,1)S(1)}, u32[]{:S(2)}, u32[]{:S(2)}) async-start(bf16[8,160,512]{2,1,0:T(8,128)(2,1)} %broadcast_in_dim.8), calls=%async_computation | async-start | bytes 2621440 | tf_op jit(solution)/shard_map/all_to_all | solution.py:23
  11.2 33.4 %copy-start.2 = (f32[128,512]{1,0:T(8,128)S(1)}, f32[128,512]{1,0:T(8,128)}, u32[]{:S(2)}) copy-start(f32[128,512]{1,0:T(8,128)} %rhs_ref.1) | copy-start | bytes 786436
  11.2 33.4 %copy-start.3 = (f32[512]{0:T(512)S(1)}, f32[512]{0:T(512)}, u32[]{:S(2)}) copy-start(f32[512]{0:T(512)} %param.11) | copy-start | bytes 6148
  11.2 33.4 %copy-start.4 = (f32[128]{0:T(128)S(1)}, f32[128]{0:T(128)}, u32[]{:S(2)}) copy-start(f32[128]{0:T(128)} %e_occ_ref.1) | copy-start | bytes 1540
  12.0 4.9 %collective-permute-start.1 = (bf16[2,160,128]{2,1,0:T(8,128)(2,1)S(1)}, bf16[2,160,128]{2,1,0:T(8,128)(2,1)S(1)}, u32[]{:S(2)}, u32[]{:S(2)}) collective-permute-start(bf16[2,160,128]{2,1,0:T(8,128)(2,1)S(1)} %pad_maximum_fusion.2), channel_id=1, source_target_pairs={{0,4},{1,5},{2,6},{3,7},{4,0},{5,1},{6,2},{7,3},{8,12},{9,13},{10,... | collective-permute-start | bytes 245768 | tf_op jit(solution)/shard_map/ppermute | solution.py:39
  17.7 4.5 %collective-permute-start.2 = (bf16[4,160,128]{2,1,0:T(8,128)(2,1)S(1)}, bf16[4,160,128]{2,1,0:T(8,128)(2,1)S(1)}, u32[]{:S(2)}, u32[]{:S(2)}) collective-permute-start(bf16[4,160,128]{2,1,0:T(8,128)(2,1)S(1)} %pad_maximum_fusion.1), channel_id=1, source_target_pairs={{0,2},{1,3},{2,0},{3,1},{4,6},{5,7},{6,4},{7,5},{8,10},{9,11},{10,... | collective-permute-start | bytes 491528 | tf_op jit(solution)/shard_map/ppermute | solution.py:39
  23.1 4.6 %collective-permute-start.3 = (bf16[8,160,128]{2,1,0:T(8,128)(2,1)S(1)}, bf16[8,160,128]{2,1,0:T(8,128)(2,1)S(1)}, u32[]{:S(2)}, u32[]{:S(2)}) collective-permute-start(bf16[8,160,128]{2,1,0:T(8,128)(2,1)S(1)} %pad_maximum_fusion), channel_id=1, source_target_pairs={{0,1},{1,0},{2,3},{3,2},{4,5},{5,4},{6,7},{7,6},{8,9},{9,8},{10,11... | collective-permute-start | bytes 983048 | tf_op jit(solution)/shard_map/ppermute | solution.py:39
  35.6 2.7 %copy-start = (bf16[2560,1280]{1,0:T(8,128)(2,1)}, bf16[2560,1280]{1,0:T(8,128)(2,1)S(1)}, u32[]{:S(2)}) copy-start(bf16[2560,1280]{1,0:T(8,128)(2,1)S(1)} %get-tuple-element.12.kern_ref) | copy-start | bytes 19660804
  38.4 16.3 %all-to-all-start.1 = ((bf16[128,4,128]{2,1,0:T(4,128)(2,1)}), bf16[128,4,128]{2,1,0:T(4,128)(2,1)S(1)}, u32[]{:S(2)}, u32[]{:S(2)}) async-start(bf16[128,4,128]{2,1,0:T(4,128)(2,1)} %get-tuple-element.10), calls=%async_computation.1 | async-start | bytes 262144 | tf_op jit(solution)/shard_map/all_to_all | solution.py:167
  69.0 2.9 %copy-start.1 = (bf16[2560,1280]{1,0:T(8,128)(2,1)S(1)}, bf16[2560,1280]{1,0:T(8,128)(2,1)}, u32[]{:S(2)}) copy-start(bf16[2560,1280]{1,0:T(8,128)(2,1)} %copy-done) | copy-start | bytes 19660804

commit v4 on v3

--- a/solution.py
+++ b/solution.py
@@ -32,11 +32,12 @@
         out_ref[pl.ds(start, tall), :] = held_ref[k]
 
 
-def gathered_by_hops(shard, axis, masks):
+def gathered_by_hops(source, shard, axis, masks):
     peers = lax.axis_size(axis)
     held, known = shard[None], [0]
-    for mask in masks:
-        other = lax.ppermute(held, axis, [(i, i ^ mask) for i in range(peers)])
+    for stage, mask in enumerate(masks):
+        sent = held if stage else source[None]
+        other = lax.ppermute(sent, axis, [(i, i ^ mask) for i in range(peers)])
         held = jnp.concatenate([held, other], 0)
         known = known + [k ^ mask for k in known]
     order = [known.index(m) for m in range(peers)]
@@ -49,28 +50,76 @@
     )(held)
 
 
-def own_kernel(e_occ_ref, rhs_ref, e_virt_ref, rhs_mine_ref, denom_ref):
-    tall, lanes = denom_ref.shape
+def stage_kernel(
+    virt_ref, occ_ref, rhs_ref, e_occ_ref, e_virt_ref,
+    copies_ref, occ_out_ref, amp_ref, rhs_mine_ref, denom_mine_ref,
+    virt_here, rhs_here, e_occ_here, e_virt_here, denom_here, sem_in, sem_out,
+):
+    pairs = (
+        (virt_ref, virt_here),
+        (rhs_ref, rhs_here),
+        (e_occ_ref, e_occ_here),
+        (e_virt_ref, e_virt_here),
+        (occ_ref, occ_out_ref),
+    )
+    fetches = [pltpu.make_async_copy(*pair, sem_in.at[i]) for i, pair in enumerate(pairs)]
+    for fetch in fetches:
+        fetch.start()
+    fetches[0].wait()
+    sends = [
+        pltpu.make_async_copy(virt_here, copies_ref.at[peer], sem_out.at[peer])
+        for peer in range(copies_ref.shape[0])
+    ]
+    for send in sends:
+        send.start()
+    for fetch in fetches[1:]:
+        fetch.wait()
+    denom = e_virt_here[...] - e_occ_here[...].T
+    denom_here[...] = denom
+    amp_ref[...] = (rhs_here[...] / denom).astype(amp_ref.dtype)
+    tall, lanes = denom_mine_ref.shape
+    parts = rhs_here.shape[1] // lanes
     mine = lax.axis_index("row") * lax.axis_size("col") + lax.axis_index("col")
-    group, part = mine // e_virt_ref.shape[0], mine % e_virt_ref.shape[0]
-    pair = rhs_ref[
-        pl.ds(pl.multiple_of(group // 2 * (2 * tall), 2 * tall), 2 * tall),
-        pl.ds(pl.multiple_of(part * lanes, lanes), lanes),
+    group, part = mine // parts, mine % parts
+    rows = pl.ds(pl.multiple_of(group // 2 * (2 * tall), 2 * tall), 2 * tall)
+    columns = pl.ds(pl.multiple_of(part * lanes, lanes), lanes)
+    for from_ref, to_ref in ((rhs_here, rhs_mine_ref), (denom_here, denom_mine_ref)):
+        pair = from_ref[rows, columns]
+        to_ref[...] = jnp.where(group % 2 == 0, pair[:tall], pair[tall:])
+    for send in sends:
+        send.wait()
+
+
+def staged(virt, occ, rhs, e_occ, e_virt, tall):
+    f32, b16 = jnp.float32, jnp.bfloat16
+    peers = lax.axis_size("row")
+    small = jax.ShapeDtypeStruct((tall, LANES), f32)
+    args = [
+        pltpu.with_memory_space_constraint(array, pltpu.HBM)
+        for array in (virt, occ, rhs, e_occ.reshape(1, -1), e_virt.reshape(1, -1))
     ]
-    rhs_mine_ref[...] = jnp.where(group % 2 == 0, pair[:tall], pair[tall:])
-    for row in range(tall):
-        denom_ref[pl.ds(row, 1), :] = e_virt_ref[pl.ds(part, 1), :] - e_occ_ref[group * tall + row]
-
-
-def own_block(rhs, e_occ, e_virt, tall):
-    small = jax.ShapeDtypeStruct((tall, LANES), jnp.float32)
-    return pl.pallas_call(
-        own_kernel,
-        out_shape=(small, small),
-        in_specs=[SMEM, VMEM, VMEM],
-        out_specs=(VMEM, VMEM),
-        compiler_params=pltpu.CompilerParams(vmem_limit_bytes=1 << 20),
-    )(e_occ, rhs, e_virt.reshape(-1, LANES))
+    return pl.pallas_call(
+        stage_kernel,
+        out_shape=(
+            jax.ShapeDtypeStruct((peers, *virt.shape), b16),
+            jax.ShapeDtypeStruct(occ.shape, b16),
+            jax.ShapeDtypeStruct(rhs.shape, b16),
+            small,
+            small,
+        ),
+        in_specs=[HBM] * 5,
+        out_specs=(HBM, VMEM, VMEM, VMEM, VMEM),
+        scratch_shapes=[
+            pltpu.VMEM(virt.shape, b16),
+            pltpu.VMEM(rhs.shape, f32),
+            pltpu.VMEM((1, rhs.shape[0]), f32),
+            pltpu.VMEM((1, rhs.shape[1]), f32),
+            pltpu.VMEM(rhs.shape, f32),
+            pltpu.SemaphoreType.DMA((5,)),
+            pltpu.SemaphoreType.DMA((peers,)),
+        ],
+        compiler_params=pltpu.CompilerParams(vmem_limit_bytes=4 << 20),
+    )(*args)
 
 
 def put_together(blocks_ref, out_ref):
@@ -153,11 +202,10 @@
     occupied, virtual = rhs.shape
     devices = lax.axis_size(BOTH)
     pieces = (devices, occupied * virtual // (devices * LANES), LANES)
-    virt_cols = sent_to_all(virt, "row").reshape(-1, virtual)
-    occ_rows = gathered_by_hops(occ, "col", (8, 4, 2, 1))
-    rhs_mine, denom_mine = own_block(rhs, e_occ, e_virt, pieces[1])
-
-    amp_b = (rhs / (e_virt[None, :] - e_occ[:, None])).astype(jnp.bfloat16)
+    copies, occ_here, amp_b, rhs_mine, denom_mine = staged(virt, occ, rhs, e_occ, e_virt, pieces[1])
+    virt_cols = lax.all_to_all(copies, "row", 0, 0, tiled=True).reshape(-1, virtual)
+    occ_rows = gathered_by_hops(occ, occ_here, "col", (8, 4, 2, 1))
+
     kernel = pltpu.with_memory_space_constraint(kernel, pltpu.HBM)
     for step in range(ITERS):
         if step == 0:

time: 106 us -> 99.5 us (0.939)
  blocking collectives: 43.5 us -> 59.8 us
  local copies, waits for them, and re-layouts: 8.66 us -> 0.17 us
  starting transfers between devices: 22.7 us -> 16.5 us
  waiting for transfers between devices: 16.5 us -> 11.2 us
  other arithmetic: 3.81 us -> 0.37 us
    all_to_all x1 -> x2, blocking collectives: 14.2 us -> 30.4 us  [body(): parts = lax.all_to_all(part, BOTH, 0, 0, tiled=True)]
    all_to_all x2 -> x1, waiting for transfers between devices: 11.9 us -> 4.71 us  [body(): lax.all_to_all(copies, 'row', 0, 0, tiled=True).reshape(-1, virtual)]
    unnamed x14 -> x4, local copies, waits for them, and re-layouts: 6.43 us -> 0.05 us
    all_to_all x2 -> x1, starting transfers between devices: 10.8 us -> 4.66 us  [body(): lax.all_to_all(copies, 'row', 0, 0, tiled=True).reshape(-1, virtual)]
    concatenate x3, other arithmetic: 2.43 us -> 0.06 us  [gathered_by_hops(): held = jnp.concatenate([held, other], 0)]
    broadcast_in_dim x3 -> x2, local copies, waits for them, and re-layouts: 2.18 us -> 0.08 us  [sent_to_all(): jnp.broadcast_to(shard[None], (peers, *shard.shape))]
    ppermute x4, waiting for transfers between devices: 4.64 us -> 6.5 us  [gathered_by_hops(): other = lax.ppermute(sent, axis, [(i, i ^ mask) for i in range(peers)])]
    pallas_call x1, Pallas kernels: 0.57 us -> 2.09 us  [staged(): pl.pallas_call(stage_kernel, out_shape=(jax.ShapeDtypeStruct((peers, *vir...]
  transfers between devices with their start and end apart: 6 -> 5, of which waited for: 5 -> 4; matrix products, arithmetic and copies ran while one was open for 6% -> 0% of each run, Pallas kernels for 1% -> 2%
where the time goes in v4:
time: 99.5 us; the launch traced here: 99.3 us
  blocking collectives  59.8 us (60%)
  starting transfers between devices  16.5 us (17%)
  Pallas kernels  11.2 us (11%)
  waiting for transfers between devices  11.2 us (11%)
    all_to_all x2, blocking collectives, body(): parts = lax.all_to_all(part, BOTH, 0, 0, tiled=True)  30.4 us
    all_to_all x2, blocking collectives, sent_to_all(): lax.all_to_all(jnp.broadcast_to(shard[None], (peers, *shard.shape)), axis...  29.3 us
    ppermute x4, starting transfers between devices, gathered_by_hops(): other = lax.ppermute(sent, axis, [(i, i ^ mask) for i in range(peers)])  11.8 us
    pallas_call x2, Pallas kernels, partial_exchange(): pl.pallas_call(functools.partial(response_kernel, cuts, 512), out_shape=(...  8.25 us
    ppermute x4, waiting for transfers between devices, gathered_by_hops(): other = lax.ppermute(sent, axis, [(i, i ^ mask) for i in range(peers)])  6.5 us
    all_to_all x1, waiting for transfers between devices, body(): lax.all_to_all(copies, 'row', 0, 0, tiled=True).reshape(-1, virtual)  4.71 us
    all_to_all x1, starting transfers between devices, body(): lax.all_to_all(copies, 'row', 0, 0, tiled=True).reshape(-1, virtual)  4.66 us
    pallas_call x1, Pallas kernels, staged(): pl.pallas_call(stage_kernel, out_shape=(jax.ShapeDtypeStruct((peers, *vir...  2.09 us
  transfers between devices with their start and end apart: 5, of which 4 were waited for; matrix products, arithmetic and copies ran while one was open for 0% of the time, Pallas kernels for 2%

profile of v4, /device:TPU:1, one launch (start us, length us, event | category | flops | bytes accessed | tf_op | source)
XLA Modules:
  0.0 99.3 jit_solution(6880096689642280863)
XLA Ops:
  0.0 4.4 %collective-permute-start = (bf16[1,160,128]{2,1,0:T(8,128)(2,1)}, bf16[1,160,128]{2,1,0:T(8,128)(2,1)S(1)}, u32[]{:S(2)}, u32[]{:S(2)}) collective-permute-start(bf16[1,160,128]{2,1,0:T(8,128)(2,1)} %bitcast.11), channel_id=1, source_target_pairs={{0,8},{1,9},{2,10},{3,11},{4,12},{5,13},{6,14},{7,15},{8,0},{9,1},... | collective-permute-start | bytes 122888 | tf_op jit(solution)/shard_map/ppermute | solution.py:40
  4.4 2.1 %shard_map.64 = (bf16[8,160,512]{2,1,0:T(8,128)(2,1)}, bf16[160,128]{1,0:T(8,128)(2,1)S(1)}, bf16[128,512]{1,0:T(8,128)(2,1)S(1)}, f32[4,128]{1,0:T(4,128)S(1)}, f32[4,128]{1,0:T(4,128)S(1)}) custom-call(bf16[160,512]{1,0:T(8,128)(2,1)} %virt_ref.1, bf16[160,128]{1,0:T(8,128)(2,1)} %occ_ref.1, f32[128,512]{1,0:T(8,128)} %rhs_ref.1, f32[1,128]{1,0:T(1,128)} %bitcast.13, ...), custom_call_target="tpu_custom_call" | custom-call | tf_op jit(solution)/shard_map/pallas_call | solution.py:101
  6.5 4.7 %all-to-all-start = ((bf16[8,160,512]{2,1,0:T(8,128)(2,1)}), bf16[8,160,512]{2,1,0:T(8,128)(2,1)S(1)}, u32[]{:S(2)}, u32[]{:S(2)}) async-start(bf16[8,160,512]{2,1,0:T(8,128)(2,1)} %get-tuple-element.14), calls=%async_computation | async-start | bytes 2621440 | tf_op jit(solution)/shard_map/all_to_all | solution.py:206
  11.2 0.0 collective-permute-done
  11.2 2.8 %collective-permute-start.1 = (bf16[2,160,128]{2,1,0:T(8,128)(2,1)S(1)}, bf16[2,160,128]{2,1,0:T(8,128)(2,1)S(1)}, u32[]{:S(2)}, u32[]{:S(2)}) collective-permute-start(bf16[2,160,128]{2,1,0:T(8,128)(2,1)S(1)} %pad_maximum_fusion.2), channel_id=1, source_target_pairs={{0,4},{1,5},{2,6},{3,7},{4,0},{5,1},{6,2},{7,3},{8,12},{9,13},{10,... | collective-permute-start | bytes 245768 | tf_op jit(solution)/shard_map/ppermute | solution.py:40
  14.0 2.1 %collective-permute-done.1 = bf16[2,160,128]{2,1,0:T(8,128)(2,1)S(1)} collective-permute-done((bf16[2,160,128]{2,1,0:T(8,128)(2,1)S(1)}, bf16[2,160,128]{2,1,0:T(8,128)(2,1)S(1)}, u32[]{:S(2)}, u32[]{:S(2)}) %collective-permute-start.1) | collective-permute-done | bytes 81952 | tf_op jit(solution)/shard_map/ppermute | solution.py:40
  16.1 1.3 %collective-permute-start.2 = (bf16[4,160,128]{2,1,0:T(8,128)(2,1)S(1)}, bf16[4,160,128]{2,1,0:T(8,128)(2,1)S(1)}, u32[]{:S(2)}, u32[]{:S(2)}) collective-permute-start(bf16[4,160,128]{2,1,0:T(8,128)(2,1)S(1)} %pad_maximum_fusion.1), channel_id=1, source_target_pairs={{0,2},{1,3},{2,0},{3,1},{4,6},{5,7},{6,4},{7,5},{8,10},{9,11},{10,... | collective-permute-start | bytes 491528 | tf_op jit(solution)/shard_map/ppermute | solution.py:40
  17.4 3.2 %collective-permute-done.2 = bf16[4,160,128]{2,1,0:T(8,128)(2,1)S(1)} collective-permute-done((bf16[4,160,128]{2,1,0:T(8,128)(2,1)S(1)}, bf16[4,160,128]{2,1,0:T(8,128)(2,1)S(1)}, u32[]{:S(2)}, u32[]{:S(2)}) %collective-permute-start.2) | collective-permute-done | bytes 163872 | tf_op jit(solution)/shard_map/ppermute | solution.py:40
  20.7 3.3 %collective-permute-start.3 = (bf16[8,160,128]{2,1,0:T(8,128)(2,1)S(1)}, bf16[8,160,128]{2,1,0:T(8,128)(2,1)S(1)}, u32[]{:S(2)}, u32[]{:S(2)}) collective-permute-start(bf16[8,160,128]{2,1,0:T(8,128)(2,1)S(1)} %pad_maximum_fusion), channel_id=1, source_target_pairs={{0,1},{1,0},{2,3},{3,2},{4,5},{5,4},{6,7},{7,6},{8,9},{9,8},{10,11... | collective-permute-start | bytes 983048 | tf_op jit(solution)/shard_map/ppermute | solution.py:40
  24.1 1.2 %collective-permute-done.3 = bf16[8,160,128]{2,1,0:T(8,128)(2,1)S(1)} collective-permute-done((bf16[8,160,128]{2,1,0:T(8,128)(2,1)S(1)}, bf16[8,160,128]{2,1,0:T(8,128)(2,1)S(1)}, u32[]{:S(2)}, u32[]{:S(2)}) %collective-permute-start.3) | collective-permute-done | bytes 327712 | tf_op jit(solution)/shard_map/ppermute | solution.py:40
  25.3 0.1 shard_map.65.occ_ref
  25.4 4.7 %all-to-all-done = bf16[8,160,512]{2,1,0:T(8,128)(2,1)S(1)} async-done(((bf16[8,160,512]{2,1,0:T(8,128)(2,1)}), bf16[8,160,512]{2,1,0:T(8,128)(2,1)S(1)}, u32[]{:S(2)}, u32[]{:S(2)}) %all-to-all-start) | async-done | bytes 1310752 | tf_op jit(solution)/shard_map/all_to_all | solution.py:206
  30.1 4.7 %shard_map.66 = (bf16[128,4,128]{2,1,0:T(4,128)(2,1)S(1)}, bf16[2560,1280]{1,0:T(8,128)(2,1)S(1)}) custom-call(bf16[128,512]{1,0:T(8,128)(2,1)S(1)} %get-tuple-element.13.amp_ref, bf16[1280,512]{1,0:T(8,128)(2,1)S(1)} %bitcast.6, bf16[2560,128]{1,0:T(8,128)(2,1)S(1)} %shard_map.65.occ_ref, bf16[2560,1280]{1,0:T(8,128)(2,1)} %kern_ref.1), custom_call_target="tpu_custom_call" | custom-call | tf_op jit(solution)/shard_map/pallas_call | solution.py:189
  34.8 16.3 %all_to_all.25 = bf16[128,4,128]{2,1,0:T(4,128)(2,1)S(1)} all-to-all(bf16[128,4,128]{2,1,0:T(4,128)(2,1)S(1)} %get-tuple-element.16), channel_id=1, replica_groups=mesh['row'=8,'col'=16] {'row','col'}, dimensions={0} | all-to-all | bytes 262144 | tf_op jit(solution)/shard_map/all_to_all | solution.py:215
  51.1 0.1 convert_reduce_fusion.1
  51.3 14.2 %all_to_all.26.amp_ref = bf16[128,4,128]{2,1,0:T(4,128)(2,1)S(1)} all-to-all(bf16[128,4,128]{2,1,0:T(4,128)(2,1)S(1)} %broadcast_in_dim.20), channel_id=1, replica_groups=mesh['row'=8,'col'=16] {'row','col'}, dimensions={0} | all-to-all | bytes 262144 | tf_op jit(solution)/shard_map/all_to_all | solution.py:23
  65.5 3.5 %shard_map.67 = bf16[128,4,128]{2,1,0:T(4,128)(2,1)S(1)} custom-call(bf16[128,4,128]{2,1,0:T(4,128)(2,1)S(1)} %all_to_all.26.amp_ref, bf16[1280,512]{1,0:T(8,128)(2,1)S(1)} %bitcast.7, bf16[2560,128]{1,0:T(8,128)(2,1)S(1)} %shard_map.65.occ_ref, bf16[2560,1280]{1,0:T(8,128)(2,1)S(1)} %get-tuple-element.18.kern_ref), custom_call_target="tpu_custom_call" | custom-call | tf_op jit(solution)/shard_map/pallas_call | solution.py:189
  69.0 14.2 %all_to_all.27 = bf16[128,4,128]{2,1,0:T(4,128)(2,1)S(1)} all-to-all(bf16[128,4,128]{2,1,0:T(4,128)(2,1)S(1)} %shard_map.67), channel_id=1, replica_groups=mesh['row'=8,'col'=16] {'row','col'}, dimensions={0} | all-to-all | bytes 262144 | tf_op jit(solution)/shard_map/all_to_all | solution.py:215
  83.1 0.1 convert_reduce_fusion
  83.3 15.2 %all_to_all.28.blocks_ref = f32[128,4,128]{2,1,0:T(4,128)S(1)} all-to-all(f32[128,4,128]{2,1,0:T(4,128)S(1)} %broadcast_in_dim.21), channel_id=1, replica_groups=mesh['row'=8,'col'=16] {'row','col'}, dimensions={0} | all-to-all | bytes 524288 | tf_op jit(solution)/shard_map/all_to_all | solution.py:23
  98.5 0.8 shard_map.68
  (12 shorter events, 0.3 us)
Async XLA Ops:
  0.0 11.2 %collective-permute-start = (bf16[1,160,128]{2,1,0:T(8,128)(2,1)}, bf16[1,160,128]{2,1,0:T(8,128)(2,1)S(1)}, u32[]{:S(2)}, u32[]{:S(2)}) collective-permute-start(bf16[1,160,128]{2,1,0:T(8,128)(2,1)} %bitcast.11), channel_id=1, source_target_pairs={{0,8},{1,9},{2,10},{3,11},{4,12},{5,13},{6,14},{7,15},{8,0},{9,1},... | collective-permute-start | bytes 122888 | tf_op jit(solution)/shard_map/ppermute | solution.py:40
  6.5 23.6 %all-to-all-start = ((bf16[8,160,512]{2,1,0:T(8,128)(2,1)}), bf16[8,160,512]{2,1,0:T(8,128)(2,1)S(1)}, u32[]{:S(2)}, u32[]{:S(2)}) async-start(bf16[8,160,512]{2,1,0:T(8,128)(2,1)} %get-tuple-element.14), calls=%async_computation | async-start | bytes 2621440 | tf_op jit(solution)/shard_map/all_to_all | solution.py:206
  11.2 4.9 %collective-permute-start.1 = (bf16[2,160,128]{2,1,0:T(8,128)(2,1)S(1)}, bf16[2,160,128]{2,1,0:T(8,128)(2,1)S(1)}, u32[]{:S(2)}, u32[]{:S(2)}) collective-permute-start(bf16[2,160,128]{2,1,0:T(8,128)(2,1)S(1)} %pad_maximum_fusion.2), channel_id=1, source_target_pairs={{0,4},{1,5},{2,6},{3,7},{4,0},{5,1},{6,2},{7,3},{8,12},{9,13},{10,... | collective-permute-start | bytes 245768 | tf_op jit(solution)/shard_map/ppermute | solution.py:40
  16.1 4.5 %collective-permute-start.2 = (bf16[4,160,128]{2,1,0:T(8,128)(2,1)S(1)}, bf16[4,160,128]{2,1,0:T(8,128)(2,1)S(1)}, u32[]{:S(2)}, u32[]{:S(2)}) collective-permute-start(bf16[4,160,128]{2,1,0:T(8,128)(2,1)S(1)} %pad_maximum_fusion.1), channel_id=1, source_target_pairs={{0,2},{1,3},{2,0},{3,1},{4,6},{5,7},{6,4},{7,5},{8,10},{9,11},{10,... | collective-permute-start | bytes 491528 | tf_op jit(solution)/shard_map/ppermute | solution.py:40
  20.7 4.6 %collective-permute-start.3 = (bf16[8,160,128]{2,1,0:T(8,128)(2,1)S(1)}, bf16[8,160,128]{2,1,0:T(8,128)(2,1)S(1)}, u32[]{:S(2)}, u32[]{:S(2)}) collective-permute-start(bf16[8,160,128]{2,1,0:T(8,128)(2,1)S(1)} %pad_maximum_fusion), channel_id=1, source_target_pairs={{0,1},{1,0},{2,3},{3,2},{4,5},{5,4},{6,7},{7,6},{8,9},{9,8},{10,11... | collective-permute-start | bytes 983048 | tf_op jit(solution)/shard_map/ppermute | solution.py:40

commit v5 on v4

--- a/solution.py
+++ b/solution.py
@@ -11,6 +11,7 @@
 ITERS = 2
 LANES = 128
 BOTH = ("row", "col")
+SEQUENCE = (2, 4, 3, 7, 6, 1, 0, 5)
 NT = (((1,), (1,)), ((), ()))
 TN = (((0,), (0,)), ((), ()))
 VMEM = pl.BlockSpec(memory_space=pltpu.VMEM)
@@ -48,6 +49,12 @@
         out_specs=VMEM,
         compiler_params=pltpu.CompilerParams(vmem_limit_bytes=4 << 20),
     )(held)
+
+
+def gathered_by_rows(copies):
+    cols = lax.axis_size("col")
+    groups = [[row * cols + col for row in SEQUENCE] for col in range(cols)]
+    return lax.all_to_all(copies, BOTH, 0, 0, tiled=True, axis_index_groups=groups)
 
 
 def stage_kernel(
@@ -127,33 +134,43 @@
     parts = out_ref.shape[1] // lanes
     for block in range(count):
         row, column = block // parts * tall, block % parts * lanes
-        out_ref[row : row + tall, column : column + lanes] = blocks_ref[block]
-
-
-def whole(blocks, shape):
-    return pl.pallas_call(
-        put_together,
-        out_shape=jax.ShapeDtypeStruct(shape, blocks.dtype),
-        in_specs=[VMEM],
+        out_ref[row : row + tall, column : column + lanes] = blocks_ref[block].astype(out_ref.dtype)
+
+
+def last_kernel(blocks_ref, rhs_ref, e_occ_ref, e_virt_ref, out_ref, exchange_ref):
+    put_together(blocks_ref, exchange_ref)
+    denom = e_virt_ref[...] - e_occ_ref[...].T
+    out_ref[...] = (rhs_ref[...] - exchange_ref[...]) / denom
+
+
+def last_amplitudes(blocks, rhs, e_occ, e_virt):
+    return pl.pallas_call(
+        last_kernel,
+        out_shape=jax.ShapeDtypeStruct(rhs.shape, jnp.float32),
+        in_specs=[VMEM] * 4,
+        scratch_shapes=[pltpu.VMEM(rhs.shape, jnp.float32)],
         compiler_params=pltpu.CompilerParams(vmem_limit_bytes=4 << 20),
-    )(blocks)
+    )(blocks, rhs, e_occ.reshape(1, -1), e_virt.reshape(1, -1))
 
 
 def response_kernel(cuts, tall, amp_ref, virt_ref, occ_ref, kern_ref, out_ref, *held):
     f32, b16 = jnp.float32, jnp.bfloat16
-    if len(amp_ref.shape) == 3:
-        *held, joined_ref = held
-        put_together(amp_ref, joined_ref)
-        amp_ref = joined_ref
     blocks = occ_ref.shape[0] // tall
     waits = {}
     if cuts:
-        held_ref, sem = held
+        held_ref, ordered_ref, sem = held
         for i, (first, last) in enumerate(zip(cuts, (*cuts[1:], blocks))):
             part = pl.ds(first * tall, (last - first) * tall)
             waits[first] = pltpu.make_async_copy(kern_ref.at[part], held_ref.at[part], sem.at[i])
             waits[first].start()
-        kern_ref = held_ref
+        share = virt_ref.shape[1]
+        for i, row in enumerate(SEQUENCE):
+            ordered_ref[row * share : (row + 1) * share, :] = virt_ref[i]
+        kern_ref, virt_ref = held_ref, ordered_ref
+    else:
+        (joined_ref,) = held
+        put_together(amp_ref, joined_ref)
+        amp_ref = joined_ref
     w = lax.dot_general(amp_ref[...], virt_ref[...], NT, preferred_element_type=f32).astype(b16)
 
     def outer_of(block):
@@ -183,41 +200,55 @@
             ].astype(out_ref.dtype)
 
 
-def partial_exchange(amp_b, virt_cols, occ_rows, kernel, pieces, cuts=()):
-    out = jax.ShapeDtypeStruct(pieces, jnp.bfloat16)
-    held = jax.ShapeDtypeStruct(kernel.shape, kernel.dtype)
+def first_exchange(amp_b, virt_blocks, occ_rows, kernel, pieces):
+    peers, share, virtual = virt_blocks.shape
+    cuts, b16 = (0, 2), jnp.bfloat16
     return pl.pallas_call(
         functools.partial(response_kernel, cuts, 512),
-        out_shape=(out, held) if cuts else out,
-        in_specs=[VMEM, VMEM, VMEM, HBM if cuts else VMEM],
-        out_specs=(VMEM, VMEM) if cuts else VMEM,
-        scratch_shapes=[pltpu.SemaphoreType.DMA((len(cuts),))]
-        if cuts
-        else [pltpu.VMEM((occ_rows.shape[1], virt_cols.shape[1]), jnp.bfloat16)],
+        out_shape=(
+            jax.ShapeDtypeStruct(pieces, b16),
+            jax.ShapeDtypeStruct(kernel.shape, b16),
+            jax.ShapeDtypeStruct((peers * share, virtual), b16),
+        ),
+        in_specs=[VMEM, VMEM, VMEM, HBM],
+        out_specs=(VMEM, VMEM, VMEM),
+        scratch_shapes=[pltpu.SemaphoreType.DMA((len(cuts),))],
         compiler_params=pltpu.CompilerParams(vmem_limit_bytes=40 << 20),
-    )(amp_b, virt_cols, occ_rows, kernel)
+    )(amp_b, virt_blocks, occ_rows, pltpu.with_memory_space_constraint(kernel, pltpu.HBM))
+
+
+def next_exchange(amp_blocks, virt_cols, occ_rows, kernel):
+    return pl.pallas_call(
+        functools.partial(response_kernel, (), 512),
+        out_shape=jax.ShapeDtypeStruct(amp_blocks.shape, jnp.bfloat16),
+        in_specs=[VMEM] * 4,
+        out_specs=VMEM,
+        scratch_shapes=[pltpu.VMEM((occ_rows.shape[1], virt_cols.shape[1]), jnp.bfloat16)],
+        compiler_params=pltpu.CompilerParams(vmem_limit_bytes=40 << 20),
+    )(amp_blocks, virt_cols, occ_rows, kernel)
 
 
 def body(kernel, occ, virt, rhs, e_occ, e_virt):
     occupied, virtual = rhs.shape
     devices = lax.axis_size(BOTH)
     pieces = (devices, occupied * virtual // (devices * LANES), LANES)
-    copies, occ_here, amp_b, rhs_mine, denom_mine = staged(virt, occ, rhs, e_occ, e_virt, pieces[1])
-    virt_cols = lax.all_to_all(copies, "row", 0, 0, tiled=True).reshape(-1, virtual)
+    copies, occ_here, amp_b, rhs_mine, denom_mine = staged(
+        virt, occ, rhs, e_occ, e_virt, pieces[1]
+    )
+    virt_blocks = gathered_by_rows(copies)
     occ_rows = gathered_by_hops(occ, occ_here, "col", (8, 4, 2, 1))
 
-    kernel = pltpu.with_memory_space_constraint(kernel, pltpu.HBM)
     for step in range(ITERS):
         if step == 0:
-            part, kernel = partial_exchange(amp_b, virt_cols, occ_rows, kernel, pieces, (0, 2))
+            part, kernel, virt_cols = first_exchange(amp_b, virt_blocks, occ_rows, kernel, pieces)
         else:
-            part = partial_exchange(amp_b, virt_cols, occ_rows, kernel, pieces)
+            part = next_exchange(amp_b, virt_cols, occ_rows, kernel)
         parts = lax.all_to_all(part, BOTH, 0, 0, tiled=True)
         exchange = jnp.sum(parts.astype(jnp.float32), axis=0)
-        amp_mine = (rhs_mine - exchange) / denom_mine
         if step < ITERS - 1:
+            amp_mine = (rhs_mine - exchange) / denom_mine
             amp_b = sent_to_all(amp_mine.astype(jnp.bfloat16), BOTH)
-    return whole(sent_to_all(amp_mine, BOTH), rhs.shape)
+    return last_amplitudes(sent_to_all(exchange.astype(jnp.bfloat16), BOTH), rhs, e_occ, e_virt)
 
 
 def solution(mesh):

time: 99.5 us -> 97.9 us (0.984)
  waiting for transfers between devices: 11.2 us -> 7.52 us
  blocking collectives: 59.8 us -> 61.1 us
    all_to_all x1, waiting for transfers between devices: 4.71 us -> 1.02 us  [gathered_by_rows(): lax.all_to_all(copies, BOTH, 0, 0, tiled=True, axis_index_groups=groups)]
    all_to_all x2, blocking collectives: 30.4 us -> 32.8 us  [body(): parts = lax.all_to_all(part, BOTH, 0, 0, tiled=True)]
    all_to_all x2, blocking collectives: 29.3 us -> 28.3 us  [sent_to_all(): lax.all_to_all(jnp.broadcast_to(shard[None], (peers, *shard.shape)), axis...]
where the time goes in v5:
time: 97.9 us; the launch traced here: 97.7 us
  blocking collectives  61.1 us (62%)
  starting transfers between devices  17.2 us (18%)
  Pallas kernels  11.3 us (12%)
  waiting for transfers between devices  7.52 us (8%)
    all_to_all x2, blocking collectives, body(): parts = lax.all_to_all(part, BOTH, 0, 0, tiled=True)  32.8 us
    all_to_all x2, blocking collectives, sent_to_all(): lax.all_to_all(jnp.broadcast_to(shard[None], (peers, *shard.shape)), axis...  28.3 us
    ppermute x4, starting transfers between devices, gathered_by_hops(): other = lax.ppermute(sent, axis, [(i, i ^ mask) for i in range(peers)])  12.1 us
    ppermute x4, waiting for transfers between devices, gathered_by_hops(): other = lax.ppermute(sent, axis, [(i, i ^ mask) for i in range(peers)])  6.5 us
    all_to_all x1, starting transfers between devices, gathered_by_rows(): lax.all_to_all(copies, BOTH, 0, 0, tiled=True, axis_index_groups=groups)  5.05 us
    pallas_call x1, Pallas kernels, first_exchange(): pl.pallas_call(functools.partial(response_kernel, cuts, 512), out_shape=(...  4.74 us
    pallas_call x1, Pallas kernels, next_exchange(): pl.pallas_call(functools.partial(response_kernel, (), 512), out_shape=jax...  3.52 us
    pallas_call x1, Pallas kernels, staged(): pl.pallas_call(stage_kernel, out_shape=(jax.ShapeDtypeStruct((peers, *vir...  2.1 us
  transfers between devices with their start and end apart: 5, of which 4 were waited for; matrix products, arithmetic and copies ran while one was open for 0% of the time, Pallas kernels for 2%

profile of v5, /device:TPU:1, one launch (start us, length us, event | category | flops | bytes accessed | tf_op | source)
XLA Modules:
  0.0 97.7 jit_solution(15122574910057498216)
XLA Ops:
  0.0 4.4 %collective-permute-start = (bf16[1,160,128]{2,1,0:T(8,128)(2,1)}, bf16[1,160,128]{2,1,0:T(8,128)(2,1)S(1)}, u32[]{:S(2)}, u32[]{:S(2)}) collective-permute-start(bf16[1,160,128]{2,1,0:T(8,128)(2,1)} %bitcast.12), channel_id=1, source_target_pairs={{0,8},{1,9},{2,10},{3,11},{4,12},{5,13},{6,14},{7,15},{8,0},{9,1},... | collective-permute-start | bytes 122888 | tf_op jit(solution)/shard_map/ppermute | solution.py:41
  4.4 2.1 %shard_map.64 = (bf16[8,160,512]{2,1,0:T(8,128)(2,1)}, bf16[160,128]{1,0:T(8,128)(2,1)S(1)}, bf16[128,512]{1,0:T(8,128)(2,1)S(1)}, f32[4,128]{1,0:T(4,128)S(1)}, f32[4,128]{1,0:T(4,128)S(1)}) custom-call(bf16[160,512]{1,0:T(8,128)(2,1)} %virt_ref.1, bf16[160,128]{1,0:T(8,128)(2,1)} %occ_ref.1, f32[128,512]{1,0:T(8,128)} %rhs_ref.3, f32[1,128]{1,0:T(1,128)} %bitcast.10, ...), custom_call_target="tpu_custom_call" | custom-call | tf_op jit(solution)/shard_map/pallas_call | solution.py:108
  6.5 5.1 %all-to-all-start = ((bf16[8,160,512]{2,1,0:T(8,128)(2,1)}), bf16[8,160,512]{2,1,0:T(8,128)(2,1)S(1)}, u32[]{:S(2)}, u32[]{:S(2)}) async-start(bf16[8,160,512]{2,1,0:T(8,128)(2,1)} %get-tuple-element.15), calls=%async_computation | async-start | bytes 2621440 | tf_op jit(solution)/shard_map/all_to_all | solution.py:57
  11.6 0.0 collective-permute-done
  11.6 2.8 %collective-permute-start.1 = (bf16[2,160,128]{2,1,0:T(8,128)(2,1)S(1)}, bf16[2,160,128]{2,1,0:T(8,128)(2,1)S(1)}, u32[]{:S(2)}, u32[]{:S(2)}) collective-permute-start(bf16[2,160,128]{2,1,0:T(8,128)(2,1)S(1)} %pad_maximum_fusion.2), channel_id=1, source_target_pairs={{0,4},{1,5},{2,6},{3,7},{4,0},{5,1},{6,2},{7,3},{8,12},{9,13},{10,... | collective-permute-start | bytes 245768 | tf_op jit(solution)/shard_map/ppermute | solution.py:41
  14.4 2.1 %collective-permute-done.1 = bf16[2,160,128]{2,1,0:T(8,128)(2,1)S(1)} collective-permute-done((bf16[2,160,128]{2,1,0:T(8,128)(2,1)S(1)}, bf16[2,160,128]{2,1,0:T(8,128)(2,1)S(1)}, u32[]{:S(2)}, u32[]{:S(2)}) %collective-permute-start.1) | collective-permute-done | bytes 81952 | tf_op jit(solution)/shard_map/ppermute | solution.py:41
  16.5 1.3 %collective-permute-start.2 = (bf16[4,160,128]{2,1,0:T(8,128)(2,1)S(1)}, bf16[4,160,128]{2,1,0:T(8,128)(2,1)S(1)}, u32[]{:S(2)}, u32[]{:S(2)}) collective-permute-start(bf16[4,160,128]{2,1,0:T(8,128)(2,1)S(1)} %pad_maximum_fusion.1), channel_id=1, source_target_pairs={{0,2},{1,3},{2,0},{3,1},{4,6},{5,7},{6,4},{7,5},{8,10},{9,11},{10,... | collective-permute-start | bytes 491528 | tf_op jit(solution)/shard_map/ppermute | solution.py:41
  17.8 3.2 %collective-permute-done.2 = bf16[4,160,128]{2,1,0:T(8,128)(2,1)S(1)} collective-permute-done((bf16[4,160,128]{2,1,0:T(8,128)(2,1)S(1)}, bf16[4,160,128]{2,1,0:T(8,128)(2,1)S(1)}, u32[]{:S(2)}, u32[]{:S(2)}) %collective-permute-start.2) | collective-permute-done | bytes 163872 | tf_op jit(solution)/shard_map/ppermute | solution.py:41
  21.1 3.6 %collective-permute-start.3 = (bf16[8,160,128]{2,1,0:T(8,128)(2,1)S(1)}, bf16[8,160,128]{2,1,0:T(8,128)(2,1)S(1)}, u32[]{:S(2)}, u32[]{:S(2)}) collective-permute-start(bf16[8,160,128]{2,1,0:T(8,128)(2,1)S(1)} %pad_maximum_fusion), channel_id=1, source_target_pairs={{0,1},{1,0},{2,3},{3,2},{4,5},{5,4},{6,7},{7,6},{8,9},{9,8},{10,11... | collective-permute-start | bytes 983048 | tf_op jit(solution)/shard_map/ppermute | solution.py:41
  24.7 1.2 %collective-permute-done.3 = bf16[8,160,128]{2,1,0:T(8,128)(2,1)S(1)} collective-permute-done((bf16[8,160,128]{2,1,0:T(8,128)(2,1)S(1)}, bf16[8,160,128]{2,1,0:T(8,128)(2,1)S(1)}, u32[]{:S(2)}, u32[]{:S(2)}) %collective-permute-start.3) | collective-permute-done | bytes 327712 | tf_op jit(solution)/shard_map/ppermute | solution.py:41
  26.0 0.1 shard_map.65.occ_ref
  26.0 1.0 %all-to-all-done.virt_ref = bf16[8,160,512]{2,1,0:T(8,128)(2,1)S(1)} async-done(((bf16[8,160,512]{2,1,0:T(8,128)(2,1)}), bf16[8,160,512]{2,1,0:T(8,128)(2,1)S(1)}, u32[]{:S(2)}, u32[]{:S(2)}) %all-to-all-start) | async-done | bytes 1310752 | tf_op jit(solution)/shard_map/all_to_all | solution.py:57
  27.1 4.7 %shard_map.66 = (bf16[128,4,128]{2,1,0:T(4,128)(2,1)S(1)}, bf16[2560,1280]{1,0:T(8,128)(2,1)S(1)}, bf16[1280,512]{1,0:T(8,128)(2,1)S(1)}) custom-call(bf16[128,512]{1,0:T(8,128)(2,1)S(1)} %get-tuple-element.14.amp_ref, bf16[8,160,512]{2,1,0:T(8,128)(2,1)S(1)} %all-to-all-done.virt_ref, bf16[2560,128]{1,0:T(8,128)(2,1)S(1)} %shard_map.65.occ_ref, ...), custom_call_target="tpu_custom_call" | custom-call | tf_op jit(solution)/shard_map/pallas_call | solution.py:206
  31.8 18.6 %all_to_all.25 = bf16[128,4,128]{2,1,0:T(4,128)(2,1)S(1)} all-to-all(bf16[128,4,128]{2,1,0:T(4,128)(2,1)S(1)} %get-tuple-element.17), channel_id=1, replica_groups=mesh['row'=8,'col'=16] {'row','col'}, dimensions={0} | all-to-all | bytes 262144 | tf_op jit(solution)/shard_map/all_to_all | solution.py:246
  50.4 0.1 convert_reduce_fusion
  50.6 14.2 %all_to_all.26.amp_ref = bf16[128,4,128]{2,1,0:T(4,128)(2,1)S(1)} all-to-all(bf16[128,4,128]{2,1,0:T(4,128)(2,1)S(1)} %broadcast_in_dim.20), channel_id=1, replica_groups=mesh['row'=8,'col'=16] {'row','col'}, dimensions={0} | all-to-all | bytes 262144 | tf_op jit(solution)/shard_map/all_to_all | solution.py:24
  64.8 0.0 copy-start
  64.8 0.0 copy-start.1
  64.8 0.0 copy-start.2
  64.8 3.5 %shard_map.67 = bf16[128,4,128]{2,1,0:T(4,128)(2,1)S(1)} custom-call(bf16[128,4,128]{2,1,0:T(4,128)(2,1)S(1)} %all_to_all.26.amp_ref, bf16[1280,512]{1,0:T(8,128)(2,1)S(1)} %get-tuple-element.19.virt_ref, bf16[2560,128]{1,0:T(8,128)(2,1)S(1)} %shard_map.65.occ_ref, bf16[2560,1280]{1,0:T(8,128)(2,1)S(1)} %get-tuple-element.20.kern_ref), custom_call_target="tpu_custom_call" | custom-call | tf_op jit(solution)/shard_map/pallas_call | solution.py:221
  68.3 14.1 %all_to_all.27 = bf16[128,4,128]{2,1,0:T(4,128)(2,1)S(1)} all-to-all(bf16[128,4,128]{2,1,0:T(4,128)(2,1)S(1)} %shard_map.67), channel_id=1, replica_groups=mesh['row'=8,'col'=16] {'row','col'}, dimensions={0} | all-to-all | bytes 262144 | tf_op jit(solution)/shard_map/all_to_all | solution.py:246
  82.5 0.1 reduce_sum.22
  82.6 14.2 %all_to_all.28.blocks_ref = bf16[128,4,128]{2,1,0:T(4,128)(2,1)S(1)} all-to-all(bf16[128,4,128]{2,1,0:T(4,128)(2,1)S(1)} %broadcast_in_dim.21), channel_id=1, replica_groups=mesh['row'=8,'col'=16] {'row','col'}, dimensions={0} | all-to-all | bytes 262144 | tf_op jit(solution)/shard_map/all_to_all | solution.py:24
  96.8 0.0 copy-done
  96.8 0.0 copy-done.1
  96.8 0.0 copy-done.2
  96.8 0.9 shard_map.68
  (11 shorter events, 0.2 us)
Async XLA Ops:
  0.0 11.6 %collective-permute-start = (bf16[1,160,128]{2,1,0:T(8,128)(2,1)}, bf16[1,160,128]{2,1,0:T(8,128)(2,1)S(1)}, u32[]{:S(2)}, u32[]{:S(2)}) collective-permute-start(bf16[1,160,128]{2,1,0:T(8,128)(2,1)} %bitcast.12), channel_id=1, source_target_pairs={{0,8},{1,9},{2,10},{3,11},{4,12},{5,13},{6,14},{7,15},{8,0},{9,1},... | collective-permute-start | bytes 122888 | tf_op jit(solution)/shard_map/ppermute | solution.py:41
  6.5 20.5 %all-to-all-start = ((bf16[8,160,512]{2,1,0:T(8,128)(2,1)}), bf16[8,160,512]{2,1,0:T(8,128)(2,1)S(1)}, u32[]{:S(2)}, u32[]{:S(2)}) async-start(bf16[8,160,512]{2,1,0:T(8,128)(2,1)} %get-tuple-element.15), calls=%async_computation | async-start | bytes 2621440 | tf_op jit(solution)/shard_map/all_to_all | solution.py:57
  11.6 4.9 %collective-permute-start.1 = (bf16[2,160,128]{2,1,0:T(8,128)(2,1)S(1)}, bf16[2,160,128]{2,1,0:T(8,128)(2,1)S(1)}, u32[]{:S(2)}, u32[]{:S(2)}) collective-permute-start(bf16[2,160,128]{2,1,0:T(8,128)(2,1)S(1)} %pad_maximum_fusion.2), channel_id=1, source_target_pairs={{0,4},{1,5},{2,6},{3,7},{4,0},{5,1},{6,2},{7,3},{8,12},{9,13},{10,... | collective-permute-start | bytes 245768 | tf_op jit(solution)/shard_map/ppermute | solution.py:41
  16.5 4.5 %collective-permute-start.2 = (bf16[4,160,128]{2,1,0:T(8,128)(2,1)S(1)}, bf16[4,160,128]{2,1,0:T(8,128)(2,1)S(1)}, u32[]{:S(2)}, u32[]{:S(2)}) collective-permute-start(bf16[4,160,128]{2,1,0:T(8,128)(2,1)S(1)} %pad_maximum_fusion.1), channel_id=1, source_target_pairs={{0,2},{1,3},{2,0},{3,1},{4,6},{5,7},{6,4},{7,5},{8,10},{9,11},{10,... | collective-permute-start | bytes 491528 | tf_op jit(solution)/shard_map/ppermute | solution.py:41
  21.1 4.9 %collective-permute-start.3 = (bf16[8,160,128]{2,1,0:T(8,128)(2,1)S(1)}, bf16[8,160,128]{2,1,0:T(8,128)(2,1)S(1)}, u32[]{:S(2)}, u32[]{:S(2)}) collective-permute-start(bf16[8,160,128]{2,1,0:T(8,128)(2,1)S(1)} %pad_maximum_fusion), channel_id=1, source_target_pairs={{0,1},{1,0},{2,3},{3,2},{4,5},{5,4},{6,7},{7,6},{8,9},{9,8},{10,11... | collective-permute-start | bytes 983048 | tf_op jit(solution)/shard_map/ppermute | solution.py:41
  64.8 32.0 %copy-start = (f32[128,512]{1,0:T(8,128)S(1)}, f32[128,512]{1,0:T(8,128)}, u32[]{:S(2)}) copy-start(f32[128,512]{1,0:T(8,128)} %rhs_ref.3) | copy-start | bytes 786436
  64.8 32.0 %copy-start.1 = (f32[512]{0:T(512)S(1)}, f32[512]{0:T(512)}, u32[]{:S(2)}) copy-start(f32[512]{0:T(512)} %param.11) | copy-start | bytes 6148
  64.8 32.0 %copy-start.2 = (f32[128]{0:T(128)S(1)}, f32[128]{0:T(128)}, u32[]{:S(2)}) copy-start(f32[128]{0:T(128)} %param.10) | copy-start | bytes 1540
